TPU v7x, 32 devices: a whole 2x2x4 slice. The times are simulated.
32 devices in a mesh: pop: 8 (over z, x), mp: 4 (over y, core).
Axes of the slice: x: 2, y: 2, z: 4, core: 2. Of those that a mesh axis runs over, the one named last changes fastest.
Arguments:
- context: bfloat16 [3072, 5120], P('pop', 'mp'), may hold values from -9 to 9
- out_weight: bfloat16 [5120, 5120], P('mp'), may hold values from -0.078125 to 0.078125
- residual: bfloat16 [3072, 5120], P('pop', 'mp'), may hold values from -6 to 6
- target: bfloat16 [3072, 5120], P('pop', 'mp'), may hold values from -9 to 9
- norm_gain: float32 [5120], replicated, may hold values from 0.5 to 1.5
- left_factors: bfloat16 [128, 5120], P('pop'), may hold values from -6 to 6
- right_factors: bfloat16 [128, 5120], P('pop'), may hold values from -8 to 8
- member_ranks: int32 [128], P('pop'), may hold values from 0 to 127, each once
Outputs:
- update: float32 [5120, 5120], P('pop', 'mp')
- fitness: float32 [128], P('pop')
- base: float32 [3072, 5120], P('pop', 'mp')
Inputs may be any that keep to these rules, and one draw needn't show every extreme that they name: `member_ranks`: each number from 0 to 127 appears exactly once.
All inputs are finite; a program needn't handle non-finite values.
Results may differ from a plain program's by a relative error of at most 0.0095.
Values may be sent and summed in bfloat16 or wider, within the bound.
A program may use at most 64 MiB of HBM per device.

v0:
```python
import functools
import math

import jax
import jax.numpy as jnp
from jax import lax
from jax.experimental import pallas as pl
from jax.experimental.pallas import tpu as pltpu
from jax.sharding import PartitionSpec as P

SIGMA = 1.0
EPSILON = 1e-06


def error_sums(stream, lifted, right_rows, gain_part, target_rows, inverse):
    hidden = stream[:, None, :] + lifted[:, :, None] * right_rows[None, :, :]
    differ = gain_part * hidden * inverse[:, :, None] - target_rows[:, None, :]
    return jnp.sum(differ * differ, axis=(0, 2))


def utility(member_ranks, count_all):
    levels = jnp.arange(count_all).astype(jnp.float32)
    ceiling = math.log(count_all / 2 + 1)
    baseline = jnp.maximum(0.0, ceiling - jnp.log(levels + 1.0))
    shaped = jnp.maximum(0.0, ceiling - jnp.log(member_ranks.astype(jnp.float32) + 1.0))
    return shaped / jnp.sum(baseline) - 1.0 / count_all


def shards(
    context, out_weight, residual, target, norm_gain, left_factors, right_factors, member_ranks
):
    tok_count = context.shape[0]
    shard_width = context.shape[1]
    full_width = out_weight.shape[1]
    factor = SIGMA / math.sqrt(full_width)
    offset = lax.axis_index("mp") * shard_width
    left_cols = lax.dynamic_slice_in_dim(left_factors, offset, shard_width, 1)
    right_cols = lax.dynamic_slice_in_dim(right_factors, offset, shard_width, 1)
    partial_value = jnp.dot(context, out_weight, preferred_element_type=jnp.float32)
    projected = lax.dot_general(
        context, left_cols, (((1,), (1,)), ((), ())), preferred_element_type=jnp.float32
    )
    summed = lax.psum_scatter(
        partial_value.astype(jnp.bfloat16), "mp", scatter_dimension=1, tiled=True
    ).astype(jnp.float32)
    stream = residual.astype(jnp.float32) + summed
    gain_part = lax.dynamic_slice_in_dim(norm_gain, offset, shard_width, 0)
    factor_f = right_cols.astype(jnp.float32)
    crossed = jnp.dot(stream, factor_f.T, precision=lax.Precision.HIGHEST)
    per_token = jnp.sum(stream * stream, axis=1)
    per_member = jnp.sum(factor_f * factor_f, axis=1)
    projected, crossed, per_token, per_member = lax.psum(
        (projected, crossed, per_token, per_member), "mp"
    )
    lifted = factor * projected
    meansq = (
        per_token[:, None] + 2.0 * lifted * crossed + lifted * lifted * per_member[None, :]
    ) / full_width
    inverse = lax.rsqrt(meansq + EPSILON)
    local_error = error_sums(
        stream, lifted, factor_f, gain_part, target.astype(jnp.float32), inverse
    )
    member_total = lax.psum(local_error, "mp")
    fitness = -member_total / (tok_count * full_width)
    everyone = lax.all_gather(fitness, "pop", axis=0, tiled=True)
    count_all = everyone.shape[0]
    average = jnp.mean(everyone)
    centre = everyone - average
    spread = jnp.sqrt(jnp.mean(centre * centre) + 1e-05)
    weight = utility(member_ranks, count_all) + (fitness - average) / spread / count_all
    weighted = (weight[:, None] * left_factors.astype(jnp.float32)).astype(jnp.bfloat16)
    weighted_rows = lax.all_to_all(weighted, "pop", split_axis=1, concat_axis=0, tiled=True)
    right_all = lax.all_gather(right_cols, "pop", axis=0, tiled=True)
    update = lax.dot_general(
        weighted_rows, right_all, (((0,), (0,)), ((), ())), preferred_element_type=jnp.float32
    ) * (math.sqrt(count_all) / SIGMA)
    return (update, fitness, stream)


BLK = 256
F32 = jnp.float32
BF = jnp.bfloat16


def nt_dot(a, b):
    return lax.dot_general(a, b, (((1,), (1,)), ((), ())), preferred_element_type=F32)


def split_two(x):
    hi = x.astype(BF)
    return hi, (x - hi.astype(F32)).astype(BF)


def row_sums(ones, acc):
    hi = acc.astype(BF)
    rest = acc - hi.astype(F32)
    mid, low = split_two(rest)
    return nt_dot(ones, hi) + nt_dot(ones, mid) + nt_dot(ones, low)


def fold_lanes(x):
    total = x[:, :128]
    for i in range(1, x.shape[1] // 128):
        total = total + x[:, i * 128:(i + 1) * 128]
    return total


def kernel(
    n_pop, n_mp, ctx_h, w_h, res_h, tgt_h, gain_h, left_h, right_h, ranks_h,
    base, weighted, right_all, fit_out,
    w_v, ctx, res, tgt, lcols, gain, right, ranks, send_a, recv_a, send_y, recv_y, send_b, recv_b,
    lall, rall, uall, mixed, sq_s, sq_a, sq_e, pre, pre_in, post, post_in, fits,
    w_sem, loc_sem, sa, ra, sy, ry, sb, rb, s_pre, r_pre, s_post, r_post,
    s_l, r_l, s_r, r_r, s_u, r_u, s_f, r_f,
):
    tok, width = ctx.shape
    mem = right.shape[0]
    full = right.shape[1]
    rows = full // n_pop
    chunks = width // BLK
    quarter = tok // n_mp
    members = mem * n_pop
    p = lax.axis_index("pop")
    q = lax.axis_index("mp")
    y = q // 2
    c = q % 2
    mate = y * 2 + (1 - c)
    across = (1 - y) * 2 + c
    diagonal = (1 - y) * 2 + (1 - c)
    blocks = (diagonal, across, mate, q)

    def remote(src, dst, ss, rs, pop, mp):
        return pltpu.make_async_remote_copy(
            src_ref=src, dst_ref=dst, send_sem=ss, recv_sem=rs,
            device_id=(pop, mp), device_id_type=pl.DeviceIdType.MESH,
        )

    def w_copy(s, k):
        start = pl.multiple_of(blocks[s] * width + k * BLK, BLK)
        return pltpu.make_async_copy(w_h.at[:, pl.ds(start, BLK)], w_v.at[s, k], w_sem.at[s, k])

    my_cols = pl.ds(pl.multiple_of(q * width, BLK), width)
    my_rows = pl.ds(pl.multiple_of(p * rows, 128), rows)
    locals_ = [
        pltpu.make_async_copy(ctx_h, ctx, loc_sem.at[0]),
        pltpu.make_async_copy(res_h, res, loc_sem.at[1]),
        pltpu.make_async_copy(tgt_h, tgt, loc_sem.at[2]),
        pltpu.make_async_copy(left_h.at[:, my_cols], lcols, loc_sem.at[3]),
        pltpu.make_async_copy(left_h.at[:, my_rows], lall.at[0], loc_sem.at[4]),
        pltpu.make_async_copy(right_h.at[:, my_cols], rall.at[0], loc_sem.at[5]),
        pltpu.make_async_copy(gain_h, gain, loc_sem.at[6]),
        pltpu.make_async_copy(right_h, right, loc_sem.at[7]),
        pltpu.make_async_copy(ranks_h, ranks, loc_sem.at[8]),
    ]
    w_copy(0, 0).start()
    locals_[0].start()
    w_copy(1, 0).start()

    barrier = pltpu.get_barrier_semaphore()
    peers = [(i, j) for i in range(n_pop) for j in range(n_mp)][1:]
    for i, j in peers:
        pl.semaphore_signal(
            barrier, inc=1, device_id=((p + i) % n_pop, (q + j) % n_mp), device_id_type=pl.DeviceIdType.MESH
        )

    def copy_a(k):
        return remote(send_a.at[k], recv_a.at[k], sa.at[k], ra.at[k], p, mate)

    def copy_y(k):
        return remote(send_y.at[k], recv_y.at[k], sy.at[k], ry.at[k], p, across)

    def copy_b(k):
        return remote(send_b.at[k], recv_b.at[k], sb.at[k], rb.at[k], p, mate)

    def copy_l(d):
        peer = (p + d) % n_pop
        cols = pl.ds(pl.multiple_of(peer * rows, 128), rows)
        return remote(left_h.at[:, cols], lall.at[d], s_l.at[d - 1], r_l.at[d - 1], peer, q)

    def copy_r(d):
        return remote(right_h.at[:, my_cols], rall.at[d], s_r.at[d - 1], r_r.at[d - 1], (p + d) % n_pop, q)

    def copy_u(d):
        return remote(uall.at[0], uall.at[d], s_u.at[d - 1], r_u.at[d - 1], (p + d) % n_pop, q)

    def copy_f(i, j):
        n = i * n_mp + j - 1
        return remote(fits.at[0, q], fits.at[i, q], s_f.at[n], r_f.at[n], (p + i) % n_pop, (q + j) % n_mp)

    def arrive_f(i, j):
        n = i * n_mp + j - 1
        source = (q + n_mp - j) % n_mp
        return remote(fits.at[i, source], fits.at[i, source], s_f.at[n], r_f.at[n], (p + n_pop - i) % n_pop, source)

    def copy_pre(d):
        peer = (q + d) % n_mp
        return remote(pre.at[peer], pre_in.at[d - 1], s_pre.at[d - 1], r_pre.at[d - 1], p, peer)

    def copy_post(d):
        peer = (q + d) % n_mp
        return remote(post.at[peer], post_in.at[d - 1], s_post.at[d - 1], r_post.at[d - 1], p, peer)

    def product(s, k):
        w_copy(s, k).wait()
        return jnp.dot(ctx[...], w_v[s, k], preferred_element_type=F32)

    locals_[0].wait()
    w_copy(0, 0).wait()
    w_copy(0, 1).start()
    w_copy(2, 0).start()
    w_copy(1, 1).start()
    w_copy(2, 1).start()
    send_a[0] = jnp.dot(ctx[...], w_v[0, 0], preferred_element_type=F32).astype(BF)
    pl.semaphore_wait(barrier, n_mp * n_pop - 1)
    copy_a(0).start()

    def far(k, carry):
        @pl.when(k + 2 < chunks)
        def _():
            for s in range(3):
                w_copy(s, k + 2).start()

        w_copy(3, k).start()

        @pl.when(k == 1)
        def _():
            for item in locals_[1:]:
                item.start()

        mine = product(1, k)

        @pl.when(k + 1 < chunks)
        def _():
            send_a[k + 1] = product(0, k + 1).astype(BF)
            copy_a(k + 1).start()

        copy_a(k).wait_recv()
        send_y[k] = (mine + recv_a[k].astype(F32)).astype(BF)
        copy_y(k).start()
        send_b[k] = product(2, k).astype(BF)
        copy_b(k).start()
        return carry

    lax.fori_loop(0, chunks, far, 0)

    for item in locals_[1:]:
        item.wait()
    uall[0] = ranks[...].astype(F32)
    for d in range(1, n_pop):
        copy_l(d).start()
        copy_r(d).start()
        copy_u(d).start()

    def near(k, carry):
        cols = pl.ds(pl.multiple_of(k * BLK, BLK), BLK)
        base[:, cols] = product(3, k) + res[:, cols].astype(F32)
        return carry

    lax.fori_loop(0, chunks, near, 0)

    ones = jnp.ones((8, 128), BF)
    gain_mine = gain[:, my_cols]
    r_mine = rall[0].astype(F32)
    gr_hi, gr_lo = split_two(r_mine * gain_mine)
    squares = jnp.zeros((quarter, 128), F32)
    for t in range(n_mp):
        part = slice(t * quarter, (t + 1) * quarter)
        target = tgt[part, :]
        pre[t, 0:mem, :] = nt_dot(lcols[...], ctx[part, :])
        pre[t, mem:2 * mem, :] = nt_dot(gr_hi, target) + nt_dot(gr_lo, target)
        wide = target.astype(F32)
        squares = squares + fold_lanes(wide * wide)
    for d in range(1, n_mp):
        copy_pre(d).start()
    t_sq = jnp.sum(jnp.sum(squares, axis=1, keepdims=True), axis=0, keepdims=True)
    g2_hi, g2_lo = split_two(r_mine * (gain_mine * gain_mine))
    for k in range(chunks):
        cols = slice(k * BLK, (k + 1) * BLK)
        mixed[k, 0:mem, :] = rall[0, :, cols]
        mixed[k, mem:2 * mem, :] = g2_hi[:, cols]
        mixed[k, 2 * mem:3 * mem, :] = g2_lo[:, cols]
    r_full = right[...].astype(F32)
    gr_full = r_full * gain[...]
    norm_r = jnp.sum(r_full * r_full, axis=1, keepdims=True)
    norm_gr = jnp.sum(gr_full * gr_full, axis=1, keepdims=True)
    sq_s[...] = jnp.zeros_like(sq_s)
    sq_a[...] = jnp.zeros_like(sq_a)
    sq_e[...] = jnp.zeros_like(sq_e)
    post[...] = jnp.zeros_like(post)

    def settle(k, carry):
        copy_b(k).wait_recv()
        copy_y(k).wait_recv()
        cols = pl.ds(pl.multiple_of(k * BLK, BLK), BLK)
        gain_k = gain[:, pl.ds(pl.multiple_of(q * width + k * BLK, BLK), BLK)]
        for t in range(n_mp):
            part = slice(t * quarter, (t + 1) * quarter)
            s = base[part, cols] + recv_b[k, part, :].astype(F32) + recv_y[k, part, :].astype(F32)
            base[part, cols] = s
            hi, low = split_two(s)
            both = nt_dot(mixed[k], hi) + nt_dot(mixed[k], low)
            post[t, 0:mem, :] += both[0:mem]
            post[t, mem:2 * mem, :] += both[mem:2 * mem] + both[2 * mem:3 * mem]
            gs = s * gain_k
            sq_s[part, :] += fold_lanes(s * s)
            sq_a[part, :] += fold_lanes(gs * gs)
            sq_e[part, :] += fold_lanes(gs * tgt[part, cols].astype(F32))
        return carry

    lax.fori_loop(0, chunks, settle, 0)
    line = lax.broadcasted_iota(jnp.int32, (8, quarter), 0)
    for t in range(n_mp):
        part = slice(t * quarter, (t + 1) * quarter)
        rest = jnp.where(line == 1, row_sums(ones, sq_a[part, :]), row_sums(ones, sq_e[part, :]))
        post[t, 2 * mem:2 * mem + 8, :] = jnp.where(line == 0, row_sums(ones, sq_s[part, :]), rest)
    for d in range(1, n_mp):
        copy_post(d).start()
    early = pre[q]
    for d in range(1, n_mp):
        copy_pre(d).wait_recv()
        early = early + pre_in[d - 1]
    late = post[q]
    for d in range(1, n_mp):
        copy_post(d).wait_recv()
        late = late + post_in[d - 1]
    lifted = early[0:mem] * (SIGMA / math.sqrt(full))
    cross_t = early[mem:2 * mem]
    crossed = late[0:mem]
    crossed_g = late[mem:2 * mem]
    s_sq = late[2 * mem:2 * mem + 1]
    a_sq = late[2 * mem + 1:2 * mem + 2]
    e_sq = late[2 * mem + 2:2 * mem + 3]
    meansq = (s_sq + 2.0 * lifted * crossed + lifted * lifted * norm_r) / full
    inverse = lax.rsqrt(meansq + EPSILON)
    power = a_sq + 2.0 * lifted * crossed_g + lifted * lifted * norm_gr
    errors = inverse * inverse * power - 2.0 * inverse * (e_sq + lifted * cross_t)
    fits[0, q] = row_sums(jnp.ones((8, quarter), BF), errors)[0:1] + t_sq
    for i, j in peers:
        copy_f(i, j).start()
    for d in range(1, n_pop):
        copy_l(d).wait_recv()
        copy_r(d).wait_recv()
        copy_u(d).wait_recv()
    for d in range(n_pop):
        right_all[d * mem:(d + 1) * mem, :] = rall[d]
    ceiling = math.log(members / 2 + 1)
    whole = sum(max(0.0, ceiling - math.log(i + 1.0)) for i in range(members))
    shaped = jnp.maximum(0.0, ceiling - jnp.log(uall[...] + 1.0)) / whole - 1.0 / members
    for i, j in peers:
        arrive_f(i, j).wait_recv()
    total = fits[:, 0]
    for j in range(1, n_mp):
        total = total + fits[:, j]
    everyone = -total / (tok * full)
    fit_out[...] = everyone[0]
    average = jnp.sum(jnp.sum(everyone, axis=0), axis=1, keepdims=True) / members
    centre = everyone - average[None]
    spread = jnp.sqrt(jnp.sum(jnp.sum(centre * centre, axis=0), axis=1, keepdims=True) / members + 1e-05)
    weight = shaped + centre / spread[None] / members
    square = (mem, mem)
    eye = lax.broadcasted_iota(jnp.int32, square, 0) == lax.broadcasted_iota(jnp.int32, square, 1)
    for d in range(n_pop):
        upright = jnp.sum(jnp.where(eye, weight[d], 0.0), axis=1, keepdims=True)
        weighted[d * mem:(d + 1) * mem, :] = (upright * lall[d].astype(F32)).astype(BF)

    def drain(k, carry):
        copy_a(k).wait_send()
        copy_y(k).wait_send()
        copy_b(k).wait_send()
        return carry

    lax.fori_loop(0, chunks, drain, 0)
    for d in range(1, n_mp):
        copy_pre(d).wait_send()
        copy_post(d).wait_send()
    for d in range(1, n_pop):
        copy_l(d).wait_send()
        copy_r(d).wait_send()
        copy_u(d).wait_send()
    for i, j in peers:
        copy_f(i, j).wait_send()


def in_hbm(x):
    return pltpu.with_memory_space_constraint(x, pltpu.HBM)


def fused_shards(
    n_pop, n_mp, context, out_weight, residual, target, norm_gain, left_factors, right_factors, member_ranks
):
    tok, width = context.shape
    full = out_weight.shape[1]
    mem = left_factors.shape[0]
    rows = full // n_pop
    chunks = width // BLK
    quarter = tok // n_mp
    ranks = member_ranks.reshape(1, mem)
    anywhere = pl.BlockSpec(memory_space=pltpu.HBM)
    vmem = pl.BlockSpec(memory_space=pltpu.VMEM)
    block = pltpu.VMEM((chunks, tok, BLK), BF)
    dma = pltpu.SemaphoreType.DMA
    acc = pltpu.VMEM((tok, 128), F32)
    base, weighted, right_all, fitness = pl.pallas_call(
        functools.partial(kernel, n_pop, n_mp),
        name="es_step",
        out_shape=(
            jax.ShapeDtypeStruct((tok, width), F32),
            jax.ShapeDtypeStruct((n_pop * mem, rows), BF),
            jax.ShapeDtypeStruct((n_pop * mem, width), BF),
            jax.ShapeDtypeStruct((1, mem), F32),
        ),
        in_specs=[anywhere] * 8,
        out_specs=[vmem] * 4,
        scratch_shapes=[
            pltpu.VMEM((4, chunks, width, BLK), BF),
            pltpu.VMEM((tok, width), BF),
            pltpu.VMEM((tok, width), BF),
            pltpu.VMEM((tok, width), BF),
            pltpu.VMEM((mem, width), BF),
            pltpu.VMEM((1, full), F32),
            pltpu.VMEM((mem, full), BF),
            pltpu.VMEM((1, mem), jnp.int32),
            block, block, block, block, block, block,
            pltpu.VMEM((n_pop, mem, rows), BF),
            pltpu.VMEM((n_pop, mem, width), BF),
            pltpu.VMEM((n_pop, 1, mem), F32),
            pltpu.VMEM((chunks, 3 * mem, BLK), BF),
            acc, acc, acc,
            pltpu.VMEM((n_mp, 2 * mem, quarter), F32),
            pltpu.VMEM((n_mp - 1, 2 * mem, quarter), F32),
            pltpu.VMEM((n_mp, 2 * mem + 8, quarter), F32),
            pltpu.VMEM((n_mp - 1, 2 * mem + 8, quarter), F32),
            pltpu.VMEM((n_pop, n_mp, 1, mem), F32),
            dma((4, chunks)),
            dma((9,)),
        ]
        + [dma((chunks,))] * 6
        + [dma((n_mp - 1,))] * 4
        + [dma((n_pop - 1,))] * 6
        + [dma((n_mp * n_pop - 1,))] * 2,
        compiler_params=pltpu.CompilerParams(
            collective_id=0, has_side_effects=True, vmem_limit_bytes=48 * 1024 * 1024
        ),
    )(
        *map(in_hbm, (
            context, out_weight, residual, target, norm_gain.reshape(1, full), left_factors,
            right_factors, ranks,
        ))
    )
    count_all = n_pop * mem
    update, base, fitness = pl.pallas_call(
        functools.partial(finish, math.sqrt(count_all) / SIGMA),
        name="es_update",
        out_shape=(
            jax.ShapeDtypeStruct((rows, width), F32),
            jax.ShapeDtypeStruct((tok, width), F32),
            jax.ShapeDtypeStruct((1, mem), F32),
        ),
        in_specs=[vmem] * 4,
        out_specs=[anywhere] * 3,
        scratch_shapes=[pltpu.VMEM((rows, width), F32), dma((rows // 128 + 2,))],
        compiler_params=pltpu.CompilerParams(vmem_limit_bytes=16 * 1024 * 1024),
    )(weighted, right_all, base, fitness)
    return (update, fitness.reshape(mem), base)


def finish(scale, weighted, right_all, base_in, fit_in, update, base, fit, held, sems):
    steps = held.shape[0] // 128
    copies = [
        pltpu.make_async_copy(base_in, base, sems.at[steps]),
        pltpu.make_async_copy(fit_in, fit, sems.at[steps + 1]),
    ]
    copies[0].start()
    copies[1].start()
    for i in range(steps):
        part = slice(i * 128, (i + 1) * 128)
        held[part, :] = lax.dot_general(
            weighted[:, part], right_all[...], (((0,), (0,)), ((), ())), preferred_element_type=F32
        ) * scale
        copies.append(pltpu.make_async_copy(held.at[part], update.at[part], sems.at[i]))
        copies[-1].start()
    for item in copies:
        item.wait()


def chosen(n_pop, n_mp, context, out_weight, *rest):
    tok, width = context.shape
    mem = rest[3].shape[0]
    full = out_weight.shape[1]
    if n_mp == 4 and width % BLK == 0 and width > BLK and (full // n_pop) % 128 == 0 and tok % (16 * n_mp) == 0 and mem % 16 == 0:
        return fused_shards(n_pop, n_mp, context, out_weight, *rest)
    return shards(context, out_weight, *rest)


def solution(mesh):
    in_specs = (
        P("pop", "mp"),
        P("mp", None),
        P("pop", "mp"),
        P("pop", "mp"),
        P(),
        P("pop", None),
        P("pop", None),
        P("pop"),
    )
    out_specs = (P("pop", "mp"), P("pop"), P("pop", "mp"))
    return jax.shard_map(
        functools.partial(chosen, mesh.shape["pop"], mesh.shape["mp"]), mesh=mesh, in_specs=in_specs, out_specs=out_specs, check_vma=False)
```

profile of v0, /device:TPU:0, one launch (start us, length us, event | category | flops | bytes accessed | tf_op | source)
XLA Modules:
  0.0 44.7 jit_solution(17526375982216431992)
XLA Ops:
  0.6 41.7 %es_step.1 = (f32[384,1280]{1,0:T(8,128)S(1)}, bf16[128,640]{1,0:T(8,128)(2,1)S(1)}, bf16[128,1280]{1,0:T(8,128)(2,1)S(1)}, f32[1,16]{1,0:T(1,128)S(1)}) custom-call(bf16[384,1280]{1,0:T(8,128)(2,1)} %ctx_h.1, bf16[1280,5120]{1,0:T(8,128)(2,1)} %w_h.1, bf16[384,1280]{1,0:T(8,128)(2,1)} %res_h.1, bf16[384,1280]{1,0:T(8,128)(2,1)} %tgt_h.1, ...), custom_call_target="tpu_custom_call" | custom-call | tf_op jit(solution)/shard_map/es_step/pallas_call | solution.py:403
  42.3 2.4 %es_update.1 = (f32[640,1280]{1,0:T(8,128)}, f32[384,1280]{1,0:T(8,128)}, f32[1,16]{1,0:T(1,128)}) custom-call(bf16[128,640]{1,0:T(8,128)(2,1)S(1)} %get-tuple-element.10.weighted, bf16[128,1280]{1,0:T(8,128)(2,1)S(1)} %get-tuple-element.11.right_all, f32[384,1280]{1,0:T(8,128)S(1)} %get-tuple-element.12.base_in, f32[1,16]{1,0:T(1,128)S(1)} %get-tuple-element.13.fit_in), custom_call_target="tpu_custom_call" | custom-call | tf_op jit(solution)/shard_map/es_update/pallas_call | solution.py:451
where the time goes:
time: 44.9 us; the launch traced here: 44.7 us
  Pallas kernels  44.1 us (98%)
  between operations  0.64 us (1%)
    pallas_call x1, Pallas kernels, fused_shards(): pl.pallas_call(functools.partial(kernel, n_pop, n_mp), name='es_step', ou...  41.7 us
    pallas_call x1, Pallas kernels, fused_shards(): pl.pallas_call(functools.partial(finish, math.sqrt(count_all) / SIGMA), n...  2.43 us

commit v1 on v0

v1 whole, which is shorter than its diff:
```python
import functools
import math

import jax
import jax.numpy as jnp
from jax import lax
from jax.experimental import pallas as pl
from jax.experimental.pallas import tpu as pltpu
from jax.sharding import PartitionSpec as P

SIGMA = 1.0
EPSILON = 1e-06


def error_sums(stream, lifted, right_rows, gain_part, target_rows, inverse):
    hidden = stream[:, None, :] + lifted[:, :, None] * right_rows[None, :, :]
    differ = gain_part * hidden * inverse[:, :, None] - target_rows[:, None, :]
    return jnp.sum(differ * differ, axis=(0, 2))


def utility(member_ranks, count_all):
    levels = jnp.arange(count_all).astype(jnp.float32)
    ceiling = math.log(count_all / 2 + 1)
    baseline = jnp.maximum(0.0, ceiling - jnp.log(levels + 1.0))
    shaped = jnp.maximum(0.0, ceiling - jnp.log(member_ranks.astype(jnp.float32) + 1.0))
    return shaped / jnp.sum(baseline) - 1.0 / count_all


def shards(
    context, out_weight, residual, target, norm_gain, left_factors, right_factors, member_ranks
):
    tok_count = context.shape[0]
    shard_width = context.shape[1]
    full_width = out_weight.shape[1]
    factor = SIGMA / math.sqrt(full_width)
    offset = lax.axis_index("mp") * shard_width
    left_cols = lax.dynamic_slice_in_dim(left_factors, offset, shard_width, 1)
    right_cols = lax.dynamic_slice_in_dim(right_factors, offset, shard_width, 1)
    partial_value = jnp.dot(context, out_weight, preferred_element_type=jnp.float32)
    projected = lax.dot_general(
        context, left_cols, (((1,), (1,)), ((), ())), preferred_element_type=jnp.float32
    )
    summed = lax.psum_scatter(
        partial_value.astype(jnp.bfloat16), "mp", scatter_dimension=1, tiled=True
    ).astype(jnp.float32)
    stream = residual.astype(jnp.float32) + summed
    gain_part = lax.dynamic_slice_in_dim(norm_gain, offset, shard_width, 0)
    factor_f = right_cols.astype(jnp.float32)
    crossed = jnp.dot(stream, factor_f.T, precision=lax.Precision.HIGHEST)
    per_token = jnp.sum(stream * stream, axis=1)
    per_member = jnp.sum(factor_f * factor_f, axis=1)
    projected, crossed, per_token, per_member = lax.psum(
        (projected, crossed, per_token, per_member), "mp"
    )
    lifted = factor * projected
    meansq = (
        per_token[:, None] + 2.0 * lifted * crossed + lifted * lifted * per_member[None, :]
    ) / full_width
    inverse = lax.rsqrt(meansq + EPSILON)
    local_error = error_sums(
        stream, lifted, factor_f, gain_part, target.astype(jnp.float32), inverse
    )
    member_total = lax.psum(local_error, "mp")
    fitness = -member_total / (tok_count * full_width)
    everyone = lax.all_gather(fitness, "pop", axis=0, tiled=True)
    count_all = everyone.shape[0]
    average = jnp.mean(everyone)
    centre = everyone - average
    spread = jnp.sqrt(jnp.mean(centre * centre) + 1e-05)
    weight = utility(member_ranks, count_all) + (fitness - average) / spread / count_all
    weighted = (weight[:, None] * left_factors.astype(jnp.float32)).astype(jnp.bfloat16)
    weighted_rows = lax.all_to_all(weighted, "pop", split_axis=1, concat_axis=0, tiled=True)
    right_all = lax.all_gather(right_cols, "pop", axis=0, tiled=True)
    update = lax.dot_general(
        weighted_rows, right_all, (((0,), (0,)), ((), ())), preferred_element_type=jnp.float32
    ) * (math.sqrt(count_all) / SIGMA)
    return (update, fitness, stream)


BLK = 256
LANES = 128
F32 = jnp.float32
BF = jnp.bfloat16


def nt_dot(a, b):
    return lax.dot_general(a, b, (((1,), (1,)), ((), ())), preferred_element_type=F32)


def split_two(x):
    hi = x.astype(BF)
    return hi, (x - hi.astype(F32)).astype(BF)


def halves(parts):
    return jnp.concatenate([piece for part in parts for piece in split_two(part)], axis=1)


def row_picker(count):
    shape = (8, count * 2 * LANES)
    owner = lax.broadcasted_iota(jnp.int32, shape, 1) // (2 * LANES)
    return jnp.where(owner == lax.broadcasted_iota(jnp.int32, shape, 0), 1.0, 0.0).astype(BF)


def flip(index, bits):
    for bit in (1, 2, 4):
        if bits & bit:
            index = index + bit - 2 * bit * ((index // bit) % 2)
    return index


def kernel(
    n_pop, n_mp, ctx_h, w_h, res_h, tgt_h, gain_h, left_h, right_h, ranks_h,
    base, weighted, right_all, fit_out,
    w_v, ctx, res, tgt, lcols, gain, right, ranks, send, recv, lall, rall,
    sq_s, sq_a, sq_e, sq_t, lin, lin_in, lin_out, lin_far, post, post_in, fits,
    w_sem, half_sem, near_sem, loc_sem, sent, r_a, r_y, r_b,
    s_lin, r_lin, s_far, r_far, s_post, r_post, s_l, r_l, s_r, r_r, s_f, r_f, rounds,
):
    tok, width = ctx.shape
    mem = right.shape[0]
    full = right.shape[1]
    rows = full // n_pop
    chunks = width // BLK
    units = width // LANES
    per = mem // n_mp
    members = mem * n_pop
    p = lax.axis_index("pop")
    q = lax.axis_index("mp")
    mate = flip(q, 1)
    across = flip(q, 2)
    diagonal = flip(q, 3)
    blocks = (diagonal, across, mate, q)

    def remote(src, dst, ss, rs, pop, mp):
        return pltpu.make_async_remote_copy(
            src_ref=src, dst_ref=dst, send_sem=ss, recv_sem=rs,
            device_id=(pop, mp), device_id_type=pl.DeviceIdType.MESH,
        )

    def signal(sem, pop, mp):
        pl.semaphore_signal(sem, inc=1, device_id=(pop, mp), device_id_type=pl.DeviceIdType.MESH)

    def w_copy(s, k):
        start = pl.multiple_of(blocks[s] * width + k * BLK, BLK)
        sem = near_sem if s == 3 else w_sem.at[s, k % 3]
        return pltpu.make_async_copy(w_h.at[:, pl.ds(start, BLK)], w_v.at[s, k], sem)

    def w_half(h):
        start = pl.multiple_of(blocks[0] * width + h * LANES, LANES)
        cols = pl.ds(h * LANES, LANES)
        return pltpu.make_async_copy(w_h.at[:, pl.ds(start, LANES)], w_v.at[0, 0, :, cols], half_sem.at[h])

    my_cols = pl.ds(pl.multiple_of(q * width, BLK), width)
    my_rows = pl.ds(pl.multiple_of(p * rows, LANES), rows)
    locals_ = [
        pltpu.make_async_copy(ctx_h, ctx, loc_sem.at[0]),
        pltpu.make_async_copy(res_h, res, loc_sem.at[1]),
        pltpu.make_async_copy(tgt_h, tgt, loc_sem.at[2]),
        pltpu.make_async_copy(left_h.at[:, my_cols], lcols, loc_sem.at[3]),
        pltpu.make_async_copy(left_h.at[:, my_rows], lall.at[0], loc_sem.at[4]),
        pltpu.make_async_copy(right_h.at[:, my_cols], rall.at[0], loc_sem.at[5]),
        pltpu.make_async_copy(gain_h, gain, loc_sem.at[6]),
        pltpu.make_async_copy(right_h, right, loc_sem.at[7]),
        pltpu.make_async_copy(ranks_h, ranks, loc_sem.at[8]),
    ]
    w_half(0).start()
    locals_[0].start()
    w_half(1).start()
    w_copy(1, 0).start()

    barrier = pltpu.get_barrier_semaphore()
    for peer in (mate, across, diagonal):
        signal(barrier, p, peer)
    for bit in (1, 2, 4):
        signal(barrier, flip(p, bit), q)

    def copy_a(first, count, n):
        cols = pl.ds(first, count)
        return remote(send.at[0, cols], recv.at[0, cols], sent, r_a.at[n], p, mate)

    def copy_y(u):
        return remote(send.at[1, u], recv.at[1, u], sent, r_y.at[u], p, across)

    def copy_b(k):
        cols = pl.ds(2 * k, 2)
        return remote(send.at[2, cols], recv.at[2, cols], sent, r_b, p, mate)

    def copy_l(d):
        peer = flip(p, d)
        cols = pl.ds(pl.multiple_of(peer * rows, LANES), rows)
        return remote(left_h.at[:, cols], lall.at[d], s_l, r_l, peer, q)

    def copy_r(d):
        return remote(right_h.at[:, my_cols], rall.at[d], s_r, r_r, flip(p, d), q)

    def copy_f(n):
        return remote(fits.at[0], fits.at[n], s_f, r_f, flip(p, n // n_mp), flip(q, n % n_mp))

    def copy_lin(i):
        return remote(lin.at[(mate, diagonal)[i]], lin_in.at[i], s_lin, r_lin, p, mate)

    def copy_post(d):
        return remote(post.at[0], post_in.at[d - 1], s_post, r_post, p, flip(q, d))

    def split_store(which, k, value):
        send[which, 2 * k] = value[:, :LANES]
        send[which, 2 * k + 1] = value[:, LANES:]

    def product(s, k):
        return jnp.dot(ctx[...], w_v[s, k], preferred_element_type=F32)

    def half(s, h):
        return jnp.dot(ctx[...], w_v[s, 0, :, h * LANES:(h + 1) * LANES], preferred_element_type=F32)

    locals_[0].wait()
    w_half(0).wait()
    w_copy(0, 1).start()
    w_copy(2, 0).start()
    w_copy(1, 1).start()
    send[0, 0] = half(0, 0).astype(BF)
    with jax.named_scope("barrier"):
        pl.semaphore_wait(barrier, 6)
    copy_a(0, 1, 0).start()
    signal(rounds.at[0], flip(p, 1), q)
    w_half(1).wait()
    send[0, 1] = half(0, 1).astype(BF)
    copy_a(1, 1, 1).start()
    w_copy(2, 1).start()
    for s in range(3):
        w_copy(s, 2).start()
    w_copy(1, 0).wait()
    first = half(1, 0)
    second = half(1, 1)
    with jax.named_scope("wait_a0"):
        copy_a(0, 1, 0).wait_recv()
    send[1, 0] = (first + recv[0, 0].astype(F32)).astype(BF)
    copy_y(0).start()
    copy_a(1, 1, 1).wait_recv()
    send[1, 1] = (second + recv[0, 1].astype(F32)).astype(BF)
    copy_y(1).start()
    w_copy(0, 1).wait()
    split_store(0, 1, product(0, 1).astype(BF))
    copy_a(2, 2, 2).start()
    w_copy(3, 0).start()
    w_copy(2, 0).wait()
    split_store(2, 0, product(2, 0).astype(BF))
    copy_b(0).start()

    def far(k, carry):
        @pl.when(k + 2 < chunks)
        def _():
            for s in range(3):
                w_copy(s, k + 2).start()

        w_copy(3, k).start()

        @pl.when(k == 1)
        def _():
            for item in locals_[1:]:
                item.start()
            pl.semaphore_wait(rounds.at[0], 1)
            signal(rounds.at[1], flip(p, 2), q)

        @pl.when(k == 2)
        def _():
            pl.semaphore_wait(rounds.at[1], 1)
            signal(rounds.at[2], flip(p, 4), q)

        @pl.when(k == 3)
        def _():
            pl.semaphore_wait(rounds.at[2], 1)
            for d in range(1, n_pop):
                copy_r(n_pop - d).start()
                copy_l(n_pop - d).start()

        w_copy(1, k).wait()
        mine = product(1, k)

        @pl.when(k + 1 < chunks)
        def _():
            w_copy(0, k + 1).wait()
            split_store(0, k + 1, product(0, k + 1).astype(BF))
            copy_a(2 * k + 2, 2, k + 2).start()

        with jax.named_scope("wait_a"):
            copy_a(2 * k, 2, k + 1).wait_recv()
        send[1, 2 * k] = (mine[:, :LANES] + recv[0, 2 * k].astype(F32)).astype(BF)
        copy_y(2 * k).start()
        send[1, 2 * k + 1] = (mine[:, LANES:] + recv[0, 2 * k + 1].astype(F32)).astype(BF)

        @pl.when(k + 1 < chunks)
        def _():
            copy_y(2 * k + 1).start()

        w_copy(2, k).wait()
        split_store(2, k, product(2, k).astype(BF))
        copy_b(k).start()
        return carry

    with jax.named_scope("far"):
        lax.fori_loop(1, chunks, far, 0)

    for item in locals_[1:]:
        item.wait()
    pltpu.make_async_copy(w_v.at[3], w_v.at[3], near_sem).wait()

    def near(k, carry):
        cols = pl.ds(pl.multiple_of(k * BLK, BLK), BLK)
        base[:, cols] = product(3, k) + res[:, cols].astype(F32)
        return carry

    with jax.named_scope("near"):
        lax.fori_loop(0, chunks, near, 0)

    with jax.named_scope("early"):
        r_mine = rall[0].astype(F32)
        gr_hi, gr_lo = split_two(r_mine * gain[:, my_cols])
        projected = nt_dot(lcols[...], ctx[...])
        cross_t = nt_dot(gr_hi, tgt[...]) + nt_dot(gr_lo, tgt[...])
        for j in range(n_mp):
            lin[j, 0:per, :] = projected[j * per:(j + 1) * per]
            lin[j, per:2 * per, :] = cross_t[j * per:(j + 1) * per]
        r_full = right[...].astype(F32)
        gr_full = r_full * gain[...]
        norm_r = jnp.sum(r_full * r_full, axis=1, keepdims=True)
        norm_gr = jnp.sum(gr_full * gr_full, axis=1, keepdims=True)
        sq_s[...] = jnp.zeros_like(sq_s)
        sq_a[...] = jnp.zeros_like(sq_a)
        sq_e[...] = jnp.zeros_like(sq_e)
        sq_t[...] = jnp.zeros_like(sq_t)

    def mixed(block, k):
        cols = pl.ds(pl.multiple_of(block * width + k * BLK, BLK), BLK)
        r = right[:, cols]
        g = gain[:, cols]
        hi, low = split_two(r.astype(F32) * (g * g))
        return jnp.concatenate([r, hi, low], axis=0)

    def linear(k, carry):
        crossed, crossed_g = carry
        near_rows = mixed(q, k)
        far_rows = mixed(across, k)
        for h in range(2):
            cols = pl.ds(pl.multiple_of(k * BLK + h * LANES, LANES), LANES)
            part = slice(h * LANES, (h + 1) * LANES)
            u = 2 * k + h
            s = base[:, cols] + recv[2, u].astype(F32)
            base[:, cols] = s
            hi, low = split_two(s)
            both = nt_dot(near_rows[:, part], hi) + nt_dot(near_rows[:, part], low) + nt_dot(far_rows[:, part], send[1, u])
            crossed = crossed + both[0:mem]
            crossed_g = crossed_g + both[mem:2 * mem] + both[2 * mem:3 * mem]
            wide = tgt[:, cols].astype(F32)
            sq_t[...] += wide * wide
        return crossed, crossed_g

    with jax.named_scope("wait_b"):
        pltpu.make_async_copy(send.at[2], recv.at[2], r_b).wait()
    with jax.named_scope("linear"):
        empty = jnp.zeros((mem, tok), F32)
        crossed, crossed_g = lax.fori_loop(0, chunks, linear, (empty, empty))
        for j in range(n_mp):
            lin[j, 2 * per:3 * per, :] = crossed[j * per:(j + 1) * per]
            lin[j, 3 * per:4 * per, :] = crossed_g[j * per:(j + 1) * per]
        copy_lin(1).start()
        copy_lin(0).start()

    def arrived(u):
        cols = pl.ds(pl.multiple_of(u * LANES, LANES), LANES)
        gain_u = gain[:, pl.ds(pl.multiple_of(q * width + u * LANES, LANES), LANES)]
        s = base[:, cols] + recv[1, u].astype(F32)
        base[:, cols] = s
        gs = s * gain_u
        return s * s, gs * gs, gs * tgt[:, cols].astype(F32)

    def settle(u, carry):
        with jax.named_scope("wait_y"):
            copy_y(u).wait_recv()
        for acc, item in zip((sq_s, sq_a, sq_e), arrived(u)):
            acc[...] += item
        return carry

    with jax.named_scope("settle0"):
        lax.fori_loop(0, 3, settle, 0)
    with jax.named_scope("wait_lin"):
        pltpu.make_async_copy(lin_in, lin_in, r_lin).wait()
    lin_out[...] = lin[across] + lin_in[1]
    copy_far = remote(lin_out, lin_far, s_far, r_far, p, across)
    copy_far.start()
    copy_y(units - 1).start()
    own = lin[q] + lin_in[0]
    with jax.named_scope("settle1"):
        lax.fori_loop(3, units - 1, settle, 0)
    before = nt_dot(row_picker(4), halves((sq_s[...], sq_a[...], sq_e[...], sq_t[...])))
    with jax.named_scope("wait_far"):
        copy_far.wait_recv()
    own = own + lin_far[...]

    def my_members(column):
        total = jnp.zeros((per, 1), F32)
        for j in range(n_mp):
            total = total + jnp.where(q == j, 1.0, 0.0) * column[j * per:(j + 1) * per]
        return total

    lifted = own[0:per] * (SIGMA / math.sqrt(full))
    square = lifted * lifted
    extra_s = 2.0 * lifted * own[2 * per:3 * per] + square * my_members(norm_r)
    extra_a = 2.0 * lifted * own[3 * per:4 * per] + square * my_members(norm_gr)
    extra_e = lifted * own[per:2 * per]
    lane = lax.broadcasted_iota(jnp.int32, (1, mem), 1)
    mine_lane = lane // per == q
    ceiling = math.log(members / 2 + 1)
    whole = sum(max(0.0, ceiling - math.log(i + 1.0)) for i in range(members))
    shaped = jnp.maximum(0.0, ceiling - jnp.log(ranks[...].astype(F32) + 1.0)) / whole - 1.0 / members
    with jax.named_scope("wait_last"):
        copy_y(units - 1).wait_recv()
    with jax.named_scope("last"):
        after = nt_dot(row_picker(3), halves(arrived(units - 1)))
        post[0] = (before + after)[0:4]
        for d in (2, 3, 1):
            copy_post(d).start()
    with jax.named_scope("wait_post"):
        pltpu.make_async_copy(post_in, post_in, r_post).wait()
    with jax.named_scope("errors"):
        late = post[0] + post_in[0] + post_in[1] + post_in[2]
        meansq = (late[0:1] + extra_s) / full
        inverse = lax.rsqrt(meansq + EPSILON)
        errors = inverse * inverse * (late[1:2] + extra_a) - 2.0 * inverse * (late[2:3] + extra_e) + late[3:4]
        summed = jnp.sum(errors, axis=1, keepdims=True)
        stacked = jnp.concatenate([summed] * n_mp, axis=0)
        square16 = (mem, mem)
        eye = lax.broadcasted_iota(jnp.int32, square16, 0) == lax.broadcasted_iota(jnp.int32, square16, 1)
        total_row = jnp.sum(jnp.where(eye, stacked, 0.0), axis=0, keepdims=True)
        fits[0, 0:1] = jnp.where(mine_lane, total_row, 0.0)
        fits[0, 1:2] = jnp.where(mine_lane, shaped, 0.0)
        for n in range(n_pop * n_mp - 1, 0, -1):
            copy_f(n).start()
    with jax.named_scope("wait_lr"):
        pltpu.make_async_copy(lall.at[pl.ds(1, n_pop - 1)], lall.at[pl.ds(1, n_pop - 1)], r_l).wait()
        pltpu.make_async_copy(rall.at[pl.ds(1, n_pop - 1)], rall.at[pl.ds(1, n_pop - 1)], r_r).wait()
    for d in range(n_pop):
        right_all[d * mem:(d + 1) * mem, :] = rall[d]
    with jax.named_scope("drain"):
        pltpu.make_async_copy(send, send, sent).wait()
        pltpu.make_async_copy(lin_in, lin_in, s_lin).wait()
        copy_far.wait_send()
        pltpu.make_async_copy(post_in, post_in, s_post).wait()
        pltpu.make_async_copy(lall.at[pl.ds(1, n_pop - 1)], lall.at[pl.ds(1, n_pop - 1)], s_l).wait()
        pltpu.make_async_copy(rall.at[pl.ds(1, n_pop - 1)], rall.at[pl.ds(1, n_pop - 1)], s_r).wait()
    others = fits.at[pl.ds(1, n_pop * n_mp - 1)]
    with jax.named_scope("wait_f"):
        pltpu.make_async_copy(others, others, r_f).wait()
    with jax.named_scope("weights"):
        rows_of = []
        for d in range(n_pop):
            total = fits[d * n_mp]
            for j in range(1, n_mp):
                total = total + fits[d * n_mp + j]
            rows_of.append(total)
        all_fit = jnp.concatenate([row[0:1] for row in rows_of], axis=0) * (-1.0 / (tok * full))
        all_shaped = jnp.concatenate([row[1:2] for row in rows_of], axis=0)
        fit_out[...] = all_fit[0:1]
        average = jnp.sum(jnp.sum(all_fit, axis=0, keepdims=True), axis=1, keepdims=True) / members
        centre = all_fit - average
        spread = jnp.sqrt(jnp.sum(jnp.sum(centre * centre, axis=0, keepdims=True), axis=1, keepdims=True) / members + 1e-05)
        weight = all_shaped + centre / spread / members
        for d in range(n_pop):
            upright = jnp.sum(jnp.where(eye, weight[d:d + 1], 0.0), axis=1, keepdims=True)
            weighted[d * mem:(d + 1) * mem, :] = (upright * lall[d].astype(F32)).astype(BF)
        pltpu.make_async_copy(others, others, s_f).wait()


def in_hbm(x):
    return pltpu.with_memory_space_constraint(x, pltpu.HBM)


def fused_shards(
    n_pop, n_mp, context, out_weight, residual, target, norm_gain, left_factors, right_factors, member_ranks
):
    tok, width = context.shape
    full = out_weight.shape[1]
    mem = left_factors.shape[0]
    rows = full // n_pop
    chunks = width // BLK
    units = width // LANES
    ranks = member_ranks.reshape(1, mem)
    anywhere = pl.BlockSpec(memory_space=pltpu.HBM)
    vmem = pl.BlockSpec(memory_space=pltpu.VMEM)
    dma = pltpu.SemaphoreType.DMA
    acc = pltpu.VMEM((tok, LANES), F32)
    group = (4 * mem // n_mp, tok)
    base, weighted, right_all, fitness = pl.pallas_call(
        functools.partial(kernel, n_pop, n_mp),
        name="es_step",
        out_shape=(
            jax.ShapeDtypeStruct((tok, width), F32),
            jax.ShapeDtypeStruct((n_pop * mem, rows), BF),
            jax.ShapeDtypeStruct((n_pop * mem, width), BF),
            jax.ShapeDtypeStruct((1, mem), F32),
        ),
        in_specs=[anywhere] * 8,
        out_specs=[vmem] * 4,
        scratch_shapes=[
            pltpu.VMEM((4, chunks, width, BLK), BF),
            pltpu.VMEM((tok, width), BF),
            pltpu.VMEM((tok, width), BF),
            pltpu.VMEM((tok, width), BF),
            pltpu.VMEM((mem, width), BF),
            pltpu.VMEM((1, full), F32),
            pltpu.VMEM((mem, full), BF),
            pltpu.VMEM((1, mem), jnp.int32),
            pltpu.VMEM((3, units, tok, LANES), BF),
            pltpu.VMEM((3, units, tok, LANES), BF),
            pltpu.VMEM((n_pop, mem, rows), BF),
            pltpu.VMEM((n_pop, mem, width), BF),
            acc, acc, acc, acc,
            pltpu.VMEM((n_mp,) + group, F32),
            pltpu.VMEM((2,) + group, F32),
            pltpu.VMEM(group, F32),
            pltpu.VMEM(group, F32),
            pltpu.VMEM((1, 4, tok), F32),
            pltpu.VMEM((n_mp - 1, 4, tok), F32),
            pltpu.VMEM((n_pop * n_mp, 2, mem), F32),
            dma((3, 3)),
            dma((2,)),
            dma,
            dma((9,)),
            dma,
            dma((chunks + 1,)),
            dma((units,)),
        ]
        + [dma] * 13
        + [pltpu.SemaphoreType.REGULAR((3,))],
        compiler_params=pltpu.CompilerParams(
            collective_id=0, has_side_effects=True, vmem_limit_bytes=48 * 1024 * 1024
        ),
    )(
        *map(in_hbm, (
            context, out_weight, residual, target, norm_gain.reshape(1, full), left_factors,
            right_factors, ranks,
        ))
    )
    count_all = n_pop * mem
    update, base, fitness = pl.pallas_call(
        functools.partial(finish, math.sqrt(count_all) / SIGMA),
        name="es_update",
        out_shape=(
            jax.ShapeDtypeStruct((rows, width), F32),
            jax.ShapeDtypeStruct((tok, width), F32),
            jax.ShapeDtypeStruct((1, mem), F32),
        ),
        in_specs=[vmem] * 4,
        out_specs=[anywhere] * 3,
        scratch_shapes=[pltpu.VMEM((rows, width), F32), dma((rows // 128 + 2,))],
        compiler_params=pltpu.CompilerParams(vmem_limit_bytes=16 * 1024 * 1024),
    )(weighted, right_all, base, fitness)
    return (update, fitness.reshape(mem), base)


def finish(scale, weighted, right_all, base_in, fit_in, update, base, fit, held, sems):
    steps = held.shape[0] // 128
    copies = [
        pltpu.make_async_copy(base_in, base, sems.at[steps]),
        pltpu.make_async_copy(fit_in, fit, sems.at[steps + 1]),
    ]
    copies[0].start()
    copies[1].start()
    for i in range(steps):
        part = slice(i * 128, (i + 1) * 128)
        held[part, :] = lax.dot_general(
            weighted[:, part], right_all[...], (((0,), (0,)), ((), ())), preferred_element_type=F32
        ) * scale
        copies.append(pltpu.make_async_copy(held.at[part], update.at[part], sems.at[i]))
        copies[-1].start()
    for item in copies:
        item.wait()


def chosen(n_pop, n_mp, context, out_weight, *rest):
    tok, width = context.shape
    mem = rest[3].shape[0]
    full = out_weight.shape[1]
    chunks = width // BLK
    if n_mp == 4 and n_pop == 8 and width % BLK == 0 and chunks > 3 and (full // n_pop) % 128 == 0 and tok % 128 == 0 and mem == 16:
        return fused_shards(n_pop, n_mp, context, out_weight, *rest)
    return shards(context, out_weight, *rest)


def solution(mesh):
    in_specs = (
        P("pop", "mp"),
        P("mp", None),
        P("pop", "mp"),
        P("pop", "mp"),
        P(),
        P("pop", None),
        P("pop", None),
        P("pop"),
    )
    out_specs = (P("pop", "mp"), P("pop"), P("pop", "mp"))
    return jax.shard_map(
        functools.partial(chosen, mesh.shape["pop"], mesh.shape["mp"]), mesh=mesh, in_specs=in_specs, out_specs=out_specs, check_vma=False)
```

time: 44.9 us -> 43.2 us (0.962)
  Pallas kernels: 44.1 us -> 42.4 us
    pallas_call x1, Pallas kernels: 41.7 us -> 39.9 us  [fused_shards(): pl.pallas_call(functools.partial(kernel, n_pop, n_mp), name='es_step', ou...]
where the time goes in v1:
time: 43.2 us; the launch traced here: 43 us
  Pallas kernels  42.4 us (98%)
  between operations  0.64 us (1%)
    pallas_call x1, Pallas kernels, fused_shards(): pl.pallas_call(functools.partial(kernel, n_pop, n_mp), name='es_step', ou...  39.9 us
    pallas_call x1, Pallas kernels, fused_shards(): pl.pallas_call(functools.partial(finish, math.sqrt(count_all) / SIGMA), n...  2.43 us

profile of v1, /device:TPU:0, one launch (start us, length us, event | category | flops | bytes accessed | tf_op | source)
XLA Modules:
  0.0 43.0 jit_solution(17740047051667654822)
XLA Ops:
  0.6 39.9 %es_step.1 = (f32[384,1280]{1,0:T(8,128)S(1)}, bf16[128,640]{1,0:T(8,128)(2,1)S(1)}, bf16[128,1280]{1,0:T(8,128)(2,1)S(1)}, f32[1,16]{1,0:T(1,128)S(1)}) custom-call(bf16[384,1280]{1,0:T(8,128)(2,1)} %ctx_h.1, bf16[1280,5120]{1,0:T(8,128)(2,1)} %w_h.1, bf16[384,1280]{1,0:T(8,128)(2,1)} %res_h.1, bf16[384,1280]{1,0:T(8,128)(2,1)} %tgt_h.1, ...), custom_call_target="tpu_custom_call" | custom-call | tf_op jit(solution)/shard_map/es_step/pallas_call | solution.py:493
  40.6 2.4 %es_update.1 = (f32[640,1280]{1,0:T(8,128)}, f32[384,1280]{1,0:T(8,128)}, f32[1,16]{1,0:T(1,128)}) custom-call(bf16[128,640]{1,0:T(8,128)(2,1)S(1)} %get-tuple-element.10.weighted, bf16[128,1280]{1,0:T(8,128)(2,1)S(1)} %get-tuple-element.11.right_all, f32[384,1280]{1,0:T(8,128)S(1)} %get-tuple-element.12.base_in, f32[1,16]{1,0:T(1,128)S(1)} %get-tuple-element.13.fit_in), custom_call_target="tpu_custom_call" | custom-call | tf_op jit(solution)/shard_map/es_update/pallas_call | solution.py:545

commit v2 on v1

v2 whole, which is shorter than its diff:
```python
import functools
import math

import jax
import jax.numpy as jnp
from jax import lax
from jax.experimental import pallas as pl
from jax.experimental.pallas import tpu as pltpu
from jax.sharding import PartitionSpec as P

SIGMA = 1.0
EPSILON = 1e-06


def error_sums(stream, lifted, right_rows, gain_part, target_rows, inverse):
    hidden = stream[:, None, :] + lifted[:, :, None] * right_rows[None, :, :]
    differ = gain_part * hidden * inverse[:, :, None] - target_rows[:, None, :]
    return jnp.sum(differ * differ, axis=(0, 2))


def utility(member_ranks, count_all):
    levels = jnp.arange(count_all).astype(jnp.float32)
    ceiling = math.log(count_all / 2 + 1)
    baseline = jnp.maximum(0.0, ceiling - jnp.log(levels + 1.0))
    shaped = jnp.maximum(0.0, ceiling - jnp.log(member_ranks.astype(jnp.float32) + 1.0))
    return shaped / jnp.sum(baseline) - 1.0 / count_all


def shards(
    context, out_weight, residual, target, norm_gain, left_factors, right_factors, member_ranks
):
    tok_count = context.shape[0]
    shard_width = context.shape[1]
    full_width = out_weight.shape[1]
    factor = SIGMA / math.sqrt(full_width)
    offset = lax.axis_index("mp") * shard_width
    left_cols = lax.dynamic_slice_in_dim(left_factors, offset, shard_width, 1)
    right_cols = lax.dynamic_slice_in_dim(right_factors, offset, shard_width, 1)
    partial_value = jnp.dot(context, out_weight, preferred_element_type=jnp.float32)
    projected = lax.dot_general(
        context, left_cols, (((1,), (1,)), ((), ())), preferred_element_type=jnp.float32
    )
    summed = lax.psum_scatter(
        partial_value.astype(jnp.bfloat16), "mp", scatter_dimension=1, tiled=True
    ).astype(jnp.float32)
    stream = residual.astype(jnp.float32) + summed
    gain_part = lax.dynamic_slice_in_dim(norm_gain, offset, shard_width, 0)
    factor_f = right_cols.astype(jnp.float32)
    crossed = jnp.dot(stream, factor_f.T, precision=lax.Precision.HIGHEST)
    per_token = jnp.sum(stream * stream, axis=1)
    per_member = jnp.sum(factor_f * factor_f, axis=1)
    projected, crossed, per_token, per_member = lax.psum(
        (projected, crossed, per_token, per_member), "mp"
    )
    lifted = factor * projected
    meansq = (
        per_token[:, None] + 2.0 * lifted * crossed + lifted * lifted * per_member[None, :]
    ) / full_width
    inverse = lax.rsqrt(meansq + EPSILON)
    local_error = error_sums(
        stream, lifted, factor_f, gain_part, target.astype(jnp.float32), inverse
    )
    member_total = lax.psum(local_error, "mp")
    fitness = -member_total / (tok_count * full_width)
    everyone = lax.all_gather(fitness, "pop", axis=0, tiled=True)
    count_all = everyone.shape[0]
    average = jnp.mean(everyone)
    centre = everyone - average
    spread = jnp.sqrt(jnp.mean(centre * centre) + 1e-05)
    weight = utility(member_ranks, count_all) + (fitness - average) / spread / count_all
    weighted = (weight[:, None] * left_factors.astype(jnp.float32)).astype(jnp.bfloat16)
    weighted_rows = lax.all_to_all(weighted, "pop", split_axis=1, concat_axis=0, tiled=True)
    right_all = lax.all_gather(right_cols, "pop", axis=0, tiled=True)
    update = lax.dot_general(
        weighted_rows, right_all, (((0,), (0,)), ((), ())), preferred_element_type=jnp.float32
    ) * (math.sqrt(count_all) / SIGMA)
    return (update, fitness, stream)


BLK = 256
LANES = 128
F32 = jnp.float32
BF = jnp.bfloat16


def nt_dot(a, b):
    return lax.dot_general(a, b, (((1,), (1,)), ((), ())), preferred_element_type=F32)


def split_two(x):
    hi = x.astype(BF)
    return hi, (x - hi.astype(F32)).astype(BF)


def halves(parts):
    return jnp.concatenate([piece for part in parts for piece in split_two(part)], axis=1)


def row_picker(count):
    shape = (8, count * 2 * LANES)
    owner = lax.broadcasted_iota(jnp.int32, shape, 1) // (2 * LANES)
    return jnp.where(owner == lax.broadcasted_iota(jnp.int32, shape, 0), 1.0, 0.0).astype(BF)


def flip(index, bits):
    for bit in (1, 2, 4):
        if bits & bit:
            index = index + bit - 2 * bit * ((index // bit) % 2)
    return index


def kernel(
    n_pop, n_mp, ctx_h, w_h, res_h, tgt_h, gain_h, left_h, right_h, ranks_h,
    base, weighted, right_all, fit_out,
    w_v, w_top, ctx, res, tgt, lcols, gain, right, ranks, send, recv, first_v, direct, lall, rall,
    sq_s, sq_a, sq_e, sq_t, lin, lin_in, lin_out, lin_far, post, post_in, fits,
    w_sem, top_sem, near_sem, loc_sem, sent, r_a, r_y, r_b, s_top, r_top, s_a0,
    s_lin, r_lin, s_far, r_far, s_post, r_post, s_l, r_l, s_r, r_r, s_f, r_f, rounds,
):
    tok, width = ctx.shape
    mem = right.shape[0]
    full = right.shape[1]
    rows = full // n_pop
    chunks = width // BLK
    units = width // LANES
    last = units - 1
    pieces = tok // LANES
    upper = tok - 64
    per = mem // 2
    members = mem * n_pop
    p = lax.axis_index("pop")
    q = lax.axis_index("mp")
    y = q // 2
    c = q % 2
    mate = flip(q, 1)
    across = flip(q, 2)
    diagonal = flip(q, 3)
    blocks = (diagonal, across, mate, q)
    other = 2 - 2 * y

    def remote(src, dst, ss, rs, pop, mp):
        return pltpu.make_async_remote_copy(
            src_ref=src, dst_ref=dst, send_sem=ss, recv_sem=rs,
            device_id=(pop, mp), device_id_type=pl.DeviceIdType.MESH,
        )

    def signal(sem, pop, mp):
        pl.semaphore_signal(sem, inc=1, device_id=(pop, mp), device_id_type=pl.DeviceIdType.MESH)

    def wait_for(ref, sem):
        pltpu.make_async_copy(ref, ref, sem).wait()

    def w_copy(s, k):
        start = pl.multiple_of(blocks[s] * width + k * BLK, BLK)
        sem = near_sem if s == 3 else w_sem.at[s, k % 3]
        return pltpu.make_async_copy(w_h.at[:, pl.ds(start, BLK)], w_v.at[s, k], sem)

    def w_first(n):
        block = (other, other + 1, diagonal, across)[n]
        start = pl.multiple_of(block * width + (n // 2) * LANES, LANES)
        return pltpu.make_async_copy(w_h.at[:, pl.ds(start, LANES)], w_top.at[n], top_sem.at[n])

    my_cols = pl.ds(pl.multiple_of(q * width, BLK), width)
    my_rows = pl.ds(pl.multiple_of(p * rows, LANES), rows)
    locals_ = [
        pltpu.make_async_copy(ctx_h.at[0:upper], ctx.at[0:upper], loc_sem.at[0]),
        pltpu.make_async_copy(ctx_h.at[upper:tok], ctx.at[upper:tok], loc_sem.at[1]),
        pltpu.make_async_copy(res_h, res, loc_sem.at[2]),
        pltpu.make_async_copy(tgt_h, tgt, loc_sem.at[3]),
        pltpu.make_async_copy(left_h.at[:, my_cols], lcols, loc_sem.at[4]),
        pltpu.make_async_copy(left_h.at[:, my_rows], lall.at[0], loc_sem.at[5]),
        pltpu.make_async_copy(right_h.at[:, my_cols], rall.at[0], loc_sem.at[6]),
        pltpu.make_async_copy(gain_h, gain, loc_sem.at[7]),
        pltpu.make_async_copy(right_h, right, loc_sem.at[8]),
        pltpu.make_async_copy(ranks_h, ranks, loc_sem.at[9]),
    ]
    w_first(0).start()
    locals_[0].start()
    locals_[1].start()
    w_first(1).start()

    barrier = pltpu.get_barrier_semaphore()
    for peer in (mate, across, diagonal):
        signal(barrier, p, peer)
    for bit in (1, 2, 4):
        signal(barrier, flip(p, bit), q)

    def copy_top():
        return remote(first_v.at[0:upper], direct.at[c], s_top, r_top, p, other)

    def copy_a(first, count, n):
        cols = pl.ds(first, count)
        return remote(send.at[0, cols], recv.at[0, cols], sent, r_a.at[n], p, mate)

    def copy_a0(core):
        if core == 1:
            return remote(first_v.at[upper:tok], recv.at[0, 0, upper:tok], s_a0, r_a.at[0], p, mate)
        return remote(send.at[0, 0], recv.at[0, 0], s_a0, r_a.at[0], p, mate)

    def copy_y0(core):
        part = slice(0 if core == 1 else upper, tok)
        return remote(send.at[1, 0, part], recv.at[1, 0, part], s_a0, r_y.at[0], p, across)

    def copy_y(first, count, n):
        cols = pl.ds(first, count)
        return remote(send.at[1, cols], recv.at[1, cols], sent, r_y.at[n], p, across)

    def copy_end(i):
        part = slice(i * LANES, (i + 1) * LANES)
        return remote(send.at[1, last, part], recv.at[1, last, part], sent, r_y.at[chunks + 1 + i], p, across)

    def copy_b(k):
        cols = pl.ds(2 * k, 2)
        return remote(send.at[2, cols], recv.at[2, cols], sent, r_b, p, mate)

    def copy_l(d):
        peer = flip(p, d)
        cols = pl.ds(pl.multiple_of(peer * rows, LANES), rows)
        return remote(left_h.at[:, cols], lall.at[d], s_l, r_l, peer, q)

    def copy_r(d):
        return remote(right_h.at[:, my_cols], rall.at[d], s_r, r_r, flip(p, d), q)

    def copy_f(n, core):
        target = flip(q, 2 * (n % 2)) - c + core
        return remote(fits.at[0], fits.at[n], s_f.at[core], r_f, flip(p, n // 2), target)

    copy_lin = remote(lin, lin_in, s_lin, r_lin, p, mate)
    copy_far = remote(lin_out, lin_far, s_far, r_far, p, across)

    def copy_post(i, d):
        return remote(post.at[i], post_in.at[d - 1, i], s_post, r_post, p, flip(q, d))

    def split_store(which, k, value):
        send[which, 2 * k] = value[:, :LANES]
        send[which, 2 * k + 1] = value[:, LANES:]

    def product(s, k):
        return jnp.dot(ctx[...], w_v[s, k], preferred_element_type=F32)

    def narrow(n, part):
        return jnp.dot(ctx[part, :], w_top[n], preferred_element_type=F32)

    everything = slice(0, tok)
    with jax.named_scope("load0"):
        locals_[0].wait()
        w_first(0).wait()
    w_first(2).start()
    w_first(3).start()
    first_v[0:upper] = narrow(0, slice(0, upper)).astype(BF)
    with jax.named_scope("barrier"):
        pl.semaphore_wait(barrier, 6)
    copy_top().start()
    signal(rounds.at[0], flip(p, 1), q)
    locals_[1].wait()
    w_first(1).wait()
    second = narrow(1, everything)

    @pl.when(c == 0)
    def _():
        send[0, 0] = second.astype(BF)
        copy_a0(0).start()

    low_rows = narrow(0, slice(upper, tok))
    first_v[upper:tok] = low_rows.astype(BF)

    @pl.when(c == 1)
    def _():
        copy_a0(1).start()

    w_copy(0, 1).start()
    w_copy(1, 1).start()

    for k in (0, 1):
        w_copy(2, k).start()
    for s in range(3):
        w_copy(s, 2).start()
    w_copy(3, 0).start()
    w_first(2).wait()
    send[0, 1] = narrow(2, everything).astype(BF)
    copy_a(1, 1, 1).start()
    w_first(3).wait()
    third = narrow(3, everything)

    with jax.named_scope("wait_a0"):
        @pl.when(c == 0)
        def _():
            copy_a0(1).wait_recv()
            send[1, 0, 0:upper] = first_v[0:upper]
            send[1, 0, upper:tok] = (low_rows + recv[0, 0, upper:tok].astype(F32)).astype(BF)
            copy_y0(0).start()

        @pl.when(c == 1)
        def _():
            copy_a0(0).wait_recv()
            send[1, 0] = (second + recv[0, 0].astype(F32)).astype(BF)
            copy_y0(1).start()

    w_copy(0, 1).wait()
    split_store(0, 1, product(0, 1).astype(BF))
    copy_a(2, 2, 2).start()
    with jax.named_scope("wait_a1"):
        copy_a(1, 1, 1).wait_recv()
    send[1, 1] = (third + recv[0, 1].astype(F32)).astype(BF)
    copy_y(1, 1, 1).start()
    w_copy(2, 0).wait()

    def far(k, carry):
        w_copy(1, k).wait()
        mine = product(1, k)
        with jax.named_scope("wait_a"):
            copy_a(2 * k, 2, k + 1).wait_recv()
        send[1, 2 * k] = (mine[:, :LANES] + recv[0, 2 * k].astype(F32)).astype(BF)
        send[1, 2 * k + 1] = (mine[:, LANES:] + recv[0, 2 * k + 1].astype(F32)).astype(BF)

        @pl.when(k + 1 < chunks)
        def _():
            copy_y(2 * k, 2, k + 1).start()

        @pl.when(k + 1 == chunks)
        def _():
            copy_y(2 * k, 1, k + 1).start()

        @pl.when(k + 2 < chunks)
        def _():
            for s in range(3):
                w_copy(s, k + 2).start()

        w_copy(3, k).start()

        @pl.when(k == 1)
        def _():
            for item in locals_[2:]:
                item.start()
            pl.semaphore_wait(rounds.at[0], 1)
            signal(rounds.at[1], flip(p, 2), q)

        @pl.when(k == 2)
        def _():
            pl.semaphore_wait(rounds.at[1], 1)
            signal(rounds.at[2], flip(p, 4), q)

        @pl.when(k == 3)
        def _():
            pl.semaphore_wait(rounds.at[2], 1)
            for d in range(1, n_pop):
                copy_r(n_pop - d).start()
                copy_l(n_pop - d).start()

        @pl.when(k + 1 < chunks)
        def _():
            w_copy(0, k + 1).wait()
            split_store(0, k + 1, product(0, k + 1).astype(BF))
            copy_a(2 * k + 2, 2, k + 2).start()

        @pl.when(k == 1)
        def _():
            split_store(2, 0, product(2, 0).astype(BF))
            copy_b(0).start()

        w_copy(2, k).wait()
        split_store(2, k, product(2, k).astype(BF))
        copy_b(k).start()
        return carry

    with jax.named_scope("far"):
        lax.fori_loop(1, chunks, far, 0)

    for item in locals_[2:]:
        item.wait()
    wait_for(w_v.at[3], near_sem)

    def near(k, carry):
        cols = pl.ds(pl.multiple_of(k * BLK, BLK), BLK)
        base[:, cols] = product(3, k) + res[:, cols].astype(F32)
        return carry

    with jax.named_scope("near"):
        lax.fori_loop(0, chunks, near, 0)

    def spread(slot, value):
        for j in range(2):
            lin[j, slot * per:(slot + 1) * per, :] = value[j * per:(j + 1) * per]

    with jax.named_scope("early"):
        r_mine = rall[0].astype(F32)
        gr_hi, gr_lo = split_two(r_mine * gain[:, my_cols])
        spread(0, nt_dot(lcols[...], ctx[...]))
        spread(1, nt_dot(gr_hi, tgt[...]) + nt_dot(gr_lo, tgt[...]))
        r_full = right[...].astype(F32)
        gr_full = r_full * gain[...]
        norm_r = jnp.sum(r_full * r_full, axis=1, keepdims=True)
        norm_gr = jnp.sum(gr_full * gr_full, axis=1, keepdims=True)
        for acc in (sq_s, sq_a, sq_e, sq_t):
            acc[...] = jnp.zeros_like(acc)

    def mixed(block, start, size):
        cols = pl.ds(pl.multiple_of(block * width + start, LANES), size)
        r = right[:, cols]
        g = gain[:, cols]
        hi, low = split_two(r.astype(F32) * (g * g))
        return jnp.concatenate([r, hi, low], axis=0)

    def linear(k, carry):
        crossed, crossed_g = carry
        near_rows = mixed(q, k * BLK, BLK)
        far_rows = mixed(across, k * BLK, BLK)
        for h in range(2):
            cols = pl.ds(pl.multiple_of(k * BLK + h * LANES, LANES), LANES)
            part = slice(h * LANES, (h + 1) * LANES)
            u = 2 * k + h
            s = base[:, cols] + recv[2, u].astype(F32)
            base[:, cols] = s
            hi, low = split_two(s)
            both = nt_dot(near_rows[:, part], hi) + nt_dot(near_rows[:, part], low) + nt_dot(far_rows[:, part], send[1, u])
            crossed = crossed + both[0:mem]
            crossed_g = crossed_g + both[mem:2 * mem] + both[2 * mem:3 * mem]
            wide = tgt[:, cols].astype(F32)
            sq_t[...] += wide * wide
        return crossed, crossed_g

    with jax.named_scope("wait_b"):
        wait_for(recv.at[2], r_b)
    with jax.named_scope("linear"):
        top = nt_dot(mixed(other, 0, LANES), first_v[0:upper]) * jnp.where(c == 1, 1.0, 0.0)
        top = jnp.concatenate([top, jnp.zeros((3 * mem, tok - upper), F32)], axis=1)
        carry = (top[0:mem], top[mem:2 * mem] + top[2 * mem:3 * mem])
        crossed, crossed_g = lax.fori_loop(0, chunks, linear, carry)
        spread(2, crossed)
        spread(3, crossed_g)

    @pl.when(c == 0)
    def _():
        copy_lin.start()
        for i in range(pieces):
            copy_end(i).start()

    def arrived(u, part):
        cols = pl.ds(pl.multiple_of(u * LANES, LANES), LANES)
        gain_u = gain[:, pl.ds(pl.multiple_of(q * width + u * LANES, LANES), LANES)]
        s = base[part, cols] + recv[1, u, part].astype(F32)
        base[part, cols] = s
        gs = s * gain_u
        return s * s, gs * gs, gs * tgt[part, cols].astype(F32)

    def settle(u, carry):
        for acc, item in zip((sq_s, sq_a, sq_e), arrived(u, everything)):
            acc[...] += item
        return carry

    with jax.named_scope("wait_y0"):
        @pl.when(c == 0)
        def _():
            wait_for(direct, r_top)
            copy_y0(0).wait_recv()
            recv[1, 0, 0:upper] = jnp.zeros((upper, LANES), BF)
            base[0:upper, 0:LANES] += direct[0].astype(F32) + direct[1].astype(F32)

        @pl.when(c == 1)
        def _():
            copy_y0(1).wait_recv()

    settle(0, 0)
    copy_y(1, 1, 1).wait_recv()
    settle(1, 0)

    @pl.when(c == 1)
    def _():
        with jax.named_scope("wait_lin"):
            copy_lin.wait_recv()
        lin_out[...] = lin[1 - y] + lin_in[1 - y]
        copy_far.start()
        for i in range(pieces):
            copy_end(i).start()

    def settle_chunk(k, carry):
        with jax.named_scope("wait_y"):
            copy_y(2 * k, 2, k + 1).wait_recv()
        settle(2 * k, 0)
        settle(2 * k + 1, 0)
        return carry

    with jax.named_scope("settle"):
        lax.fori_loop(1, chunks - 1, settle_chunk, 0)
    with jax.named_scope("wait_y8"):
        copy_y(last - 1, 1, chunks).wait_recv()
    settle(last - 1, 0)
    before = nt_dot(row_picker(4), halves((sq_s[...], sq_a[...], sq_e[...], sq_t[...])))
    lane = lax.broadcasted_iota(jnp.int32, (1, mem), 1)
    mine_lane = lane // per == y
    ceiling = math.log(members / 2 + 1)
    whole = sum(max(0.0, ceiling - math.log(i + 1.0)) for i in range(members))
    shaped = jnp.maximum(0.0, ceiling - jnp.log(ranks[...].astype(F32) + 1.0)) / whole - 1.0 / members
    picker = row_picker(3)
    for i in range(pieces):
        part = slice(i * LANES, (i + 1) * LANES)
        with jax.named_scope("wait_end"):
            copy_end(i).wait_recv()
        with jax.named_scope("end"):
            post[i] = (before[:, part] + nt_dot(picker, halves(arrived(last, part))))[0:4]

            @pl.when(c == 0)
            def _():
                copy_post(i, 3).start()
                copy_post(i, 1).start()

            @pl.when(c == 1)
            def _():
                copy_post(i, 2).start()

    square = (mem, mem)
    eye = lax.broadcasted_iota(jnp.int32, square, 0) == lax.broadcasted_iota(jnp.int32, square, 1)
    half_of = slice(1, n_pop)
    others = fits.at[pl.ds(1, 2 * n_pop - 1)]

    @pl.when(c == 1)
    def _():
        with jax.named_scope("wait_far"):
            copy_far.wait_recv()
        own = lin[y] + lin_in[y] + lin_far[...]
        mine = jnp.where(y == 1, 1.0, 0.0)

        def my_members(column):
            return column[0:per] + mine * (column[per:mem] - column[0:per])

        lifted = own[0:per] * (SIGMA / math.sqrt(full))
        lifted2 = lifted * lifted
        extra_s = 2.0 * lifted * own[2 * per:3 * per] + lifted2 * my_members(norm_r)
        extra_a = 2.0 * lifted * own[3 * per:4 * per] + lifted2 * my_members(norm_gr)
        extra_e = lifted * own[per:2 * per]
        with jax.named_scope("wait_post"):
            wait_for(post_in, r_post)
        with jax.named_scope("errors"):
            late = jnp.concatenate([post[i] + post_in[0, i] + post_in[1, i] + post_in[2, i] for i in range(pieces)], axis=1)
            meansq = (late[0:1] + extra_s) / full
            inverse = lax.rsqrt(meansq + EPSILON)
            errors = inverse * inverse * (late[1:2] + extra_a) - 2.0 * inverse * (late[2:3] + extra_e) + late[3:4]
            summed = jnp.sum(errors, axis=1, keepdims=True)
            stacked = jnp.concatenate([summed, summed], axis=0)
            total_row = jnp.sum(jnp.where(eye, stacked, 0.0), axis=0, keepdims=True)
            fits[0, 0:1] = jnp.where(mine_lane, total_row, 0.0)
            fits[0, 1:2] = jnp.where(mine_lane, shaped, 0.0)
            for n in range(2 * n_pop - 1, -1, -1):
                copy_f(n, 0).start()
                if n > 0:
                    copy_f(n, 1).start()

    with jax.named_scope("wait_lr"):
        wait_for(lall.at[half_of], r_l)
        wait_for(rall.at[half_of], r_r)
    for d in range(n_pop):
        right_all[d * mem:(d + 1) * mem, :] = rall[d]
    with jax.named_scope("drain"):
        for which in range(3):
            wait_for(send.at[which, 1:units], sent)
        wait_for(send.at[2, 0], sent)
        wait_for(first_v.at[0:upper], s_top)
        wait_for(lall.at[half_of], s_l)
        wait_for(rall.at[half_of], s_r)

        @pl.when(c == 0)
        def _():
            copy_a0(0).wait_send()
            copy_y0(0).wait_send()
            copy_lin.wait_send()
            wait_for(post_in.at[0:2], s_post)
            with jax.named_scope("wait_f"):
                wait_for(fits, r_f)

        @pl.when(c == 1)
        def _():
            copy_a0(1).wait_send()
            copy_y0(1).wait_send()
            copy_far.wait_send()
            wait_for(post_in.at[0], s_post)
            with jax.named_scope("wait_f"):
                wait_for(others, r_f)
            wait_for(fits, s_f.at[0])
            wait_for(others, s_f.at[1])

    with jax.named_scope("weights"):
        rows_of = [fits[2 * d] + fits[2 * d + 1] for d in range(n_pop)]
        all_fit = jnp.concatenate([row[0:1] for row in rows_of], axis=0) * (-1.0 / (tok * full))
        all_shaped = jnp.concatenate([row[1:2] for row in rows_of], axis=0)
        fit_out[...] = all_fit[0:1]
        average = jnp.sum(jnp.sum(all_fit, axis=0, keepdims=True), axis=1, keepdims=True) / members
        centre = all_fit - average
        deviation = jnp.sqrt(jnp.sum(jnp.sum(centre * centre, axis=0, keepdims=True), axis=1, keepdims=True) / members + 1e-05)
        weight = all_shaped + centre / deviation / members
        for d in range(n_pop):
            upright = jnp.sum(jnp.where(eye, weight[d:d + 1], 0.0), axis=1, keepdims=True)
            weighted[d * mem:(d + 1) * mem, :] = (upright * lall[d].astype(F32)).astype(BF)


def in_hbm(x):
    return pltpu.with_memory_space_constraint(x, pltpu.HBM)


def fused_shards(
    n_pop, n_mp, context, out_weight, residual, target, norm_gain, left_factors, right_factors, member_ranks
):
    tok, width = context.shape
    full = out_weight.shape[1]
    mem = left_factors.shape[0]
    rows = full // n_pop
    chunks = width // BLK
    units = width // LANES
    pieces = tok // LANES
    ranks = member_ranks.reshape(1, mem)
    anywhere = pl.BlockSpec(memory_space=pltpu.HBM)
    vmem = pl.BlockSpec(memory_space=pltpu.VMEM)
    dma = pltpu.SemaphoreType.DMA
    acc = pltpu.VMEM((tok, LANES), F32)
    group = (2 * mem, tok)
    base, weighted, right_all, fitness = pl.pallas_call(
        functools.partial(kernel, n_pop, n_mp),
        name="es_step",
        out_shape=(
            jax.ShapeDtypeStruct((tok, width), F32),
            jax.ShapeDtypeStruct((n_pop * mem, rows), BF),
            jax.ShapeDtypeStruct((n_pop * mem, width), BF),
            jax.ShapeDtypeStruct((1, mem), F32),
        ),
        in_specs=[anywhere] * 8,
        out_specs=[vmem] * 4,
        scratch_shapes=[
            pltpu.VMEM((4, chunks, width, BLK), BF),
            pltpu.VMEM((4, width, LANES), BF),
            pltpu.VMEM((tok, width), BF),
            pltpu.VMEM((tok, width), BF),
            pltpu.VMEM((tok, width), BF),
            pltpu.VMEM((mem, width), BF),
            pltpu.VMEM((1, full), F32),
            pltpu.VMEM((mem, full), BF),
            pltpu.VMEM((1, mem), jnp.int32),
            pltpu.VMEM((3, units, tok, LANES), BF),
            pltpu.VMEM((3, units, tok, LANES), BF),
            pltpu.VMEM((tok, LANES), BF),
            pltpu.VMEM((2, tok - 64, LANES), BF),
            pltpu.VMEM((n_pop, mem, rows), BF),
            pltpu.VMEM((n_pop, mem, width), BF),
            acc, acc, acc, acc,
            pltpu.VMEM((2,) + group, F32),
            pltpu.VMEM((2,) + group, F32),
            pltpu.VMEM(group, F32),
            pltpu.VMEM(group, F32),
            pltpu.VMEM((pieces, 4, LANES), F32),
            pltpu.VMEM((n_mp - 1, pieces, 4, LANES), F32),
            pltpu.VMEM((2 * n_pop, 2, mem), F32),
            dma((3, 3)),
            dma((4,)),
            dma,
            dma((10,)),
            dma,
            dma((chunks + 1,)),
            dma((chunks + 1 + pieces,)),
        ]
        + [dma] * 14
        + [dma((2,)), dma]
        + [pltpu.SemaphoreType.REGULAR((3,))],
        compiler_params=pltpu.CompilerParams(
            collective_id=0, has_side_effects=True, vmem_limit_bytes=48 * 1024 * 1024
        ),
    )(
        *map(in_hbm, (
            context, out_weight, residual, target, norm_gain.reshape(1, full), left_factors,
            right_factors, ranks,
        ))
    )
    count_all = n_pop * mem
    update, base, fitness = pl.pallas_call(
        functools.partial(finish, math.sqrt(count_all) / SIGMA),
        name="es_update",
        out_shape=(
            jax.ShapeDtypeStruct((rows, width), F32),
            jax.ShapeDtypeStruct((tok, width), F32),
            jax.ShapeDtypeStruct((1, mem), F32),
        ),
        in_specs=[vmem] * 4,
        out_specs=[anywhere] * 3,
        scratch_shapes=[pltpu.VMEM((rows, width), F32), dma((rows // 128 + 2,))],
        compiler_params=pltpu.CompilerParams(vmem_limit_bytes=16 * 1024 * 1024),
    )(weighted, right_all, base, fitness)
    return (update, fitness.reshape(mem), base)


def finish(scale, weighted, right_all, base_in, fit_in, update, base, fit, held, sems):
    steps = held.shape[0] // 128
    copies = [
        pltpu.make_async_copy(base_in, base, sems.at[steps]),
        pltpu.make_async_copy(fit_in, fit, sems.at[steps + 1]),
    ]
    copies[0].start()
    copies[1].start()
    for i in range(steps):
        part = slice(i * 128, (i + 1) * 128)
        held[part, :] = lax.dot_general(
            weighted[:, part], right_all[...], (((0,), (0,)), ((), ())), preferred_element_type=F32
        ) * scale
        copies.append(pltpu.make_async_copy(held.at[part], update.at[part], sems.at[i]))
        copies[-1].start()
    for item in copies:
        item.wait()


def chosen(n_pop, n_mp, context, out_weight, *rest):
    tok, width = context.shape
    mem = rest[3].shape[0]
    full = out_weight.shape[1]
    chunks = width // BLK
    if n_mp == 4 and n_pop == 8 and width % BLK == 0 and chunks > 3 and (full // n_pop) % 128 == 0 and tok % 128 == 0 and mem == 16:
        return fused_shards(n_pop, n_mp, context, out_weight, *rest)
    return shards(context, out_weight, *rest)


def solution(mesh):
    in_specs = (
        P("pop", "mp"),
        P("mp", None),
        P("pop", "mp"),
        P("pop", "mp"),
        P(),
        P("pop", None),
        P("pop", None),
        P("pop"),
    )
    out_specs = (P("pop", "mp"), P("pop"), P("pop", "mp"))
    return jax.shard_map(
        functools.partial(chosen, mesh.shape["pop"], mesh.shape["mp"]), mesh=mesh, in_specs=in_specs, out_specs=out_specs, check_vma=False)
```

time: 43.2 us -> 41.1 us (0.951)
  Pallas kernels: 42.4 us -> 40.3 us
    pallas_call x1, Pallas kernels: 39.9 us -> 37.9 us  [fused_shards(): pl.pallas_call(functools.partial(kernel, n_pop, n_mp), name='es_step', ou...]
where the time goes in v2:
time: 41.1 us; the launch traced here: 41 us
  Pallas kernels  40.3 us (98%)
  between operations  0.64 us (2%)
    pallas_call x1, Pallas kernels, fused_shards(): pl.pallas_call(functools.partial(kernel, n_pop, n_mp), name='es_step', ou...  37.9 us
    pallas_call x1, Pallas kernels, fused_shards(): pl.pallas_call(functools.partial(finish, math.sqrt(count_all) / SIGMA), n...  2.43 us

profile of v2, /device:TPU:0, one launch (start us, length us, event | category | flops | bytes accessed | tf_op | source)
XLA Modules:
  0.0 41.0 jit_solution(1698675564492497974)
XLA Ops:
  0.6 37.9 %es_step.1 = (f32[384,1280]{1,0:T(8,128)S(1)}, bf16[128,640]{1,0:T(8,128)(2,1)S(1)}, bf16[128,1280]{1,0:T(8,128)(2,1)S(1)}, f32[1,16]{1,0:T(1,128)S(1)}) custom-call(bf16[384,1280]{1,0:T(8,128)(2,1)} %ctx_h.1, bf16[1280,5120]{1,0:T(8,128)(2,1)} %w_h.1, bf16[384,1280]{1,0:T(8,128)(2,1)} %res_h.1, bf16[384,1280]{1,0:T(8,128)(2,1)} %tgt_h.1, ...), custom_call_target="tpu_custom_call" | custom-call | tf_op jit(solution)/shard_map/es_step/pallas_call | solution.py:615
  38.5 2.4 %es_update.1 = (f32[640,1280]{1,0:T(8,128)}, f32[384,1280]{1,0:T(8,128)}, f32[1,16]{1,0:T(1,128)}) custom-call(bf16[128,640]{1,0:T(8,128)(2,1)S(1)} %get-tuple-element.10.weighted, bf16[128,1280]{1,0:T(8,128)(2,1)S(1)} %get-tuple-element.11.right_all, f32[384,1280]{1,0:T(8,128)S(1)} %get-tuple-element.12.base_in, f32[1,16]{1,0:T(1,128)S(1)} %get-tuple-element.13.fit_in), custom_call_target="tpu_custom_call" | custom-call | tf_op jit(solution)/shard_map/es_update/pallas_call | solution.py:671

commit v3 on v2

--- a/solution.py
+++ b/solution.py
@@ -112,10 +112,9 @@
 def kernel(
     n_pop, n_mp, ctx_h, w_h, res_h, tgt_h, gain_h, left_h, right_h, ranks_h,
     base, weighted, right_all, fit_out,
-    w_v, w_top, ctx, res, tgt, lcols, gain, right, ranks, send, recv, first_v, direct, lall, rall,
+    w_v, ctx, res, tgt, lcols, gain, right, ranks, send, recv, first_v, direct, lall, rall,
     sq_s, sq_a, sq_e, sq_t, lin, lin_in, lin_out, lin_far, post, post_in, fits,
-    w_sem, top_sem, near_sem, loc_sem, sent, r_a, r_y, r_b, s_top, r_top, s_a0,
-    s_lin, r_lin, s_far, r_far, s_post, r_post, s_l, r_l, s_r, r_r, s_f, r_f, rounds,
+    w_sem, top_sem, near_sem, loc_sem, sent, r_a, r_y, r_b, r_top, r_lin, r_far, r_post, r_l, r_r, r_f, rounds,
 ):
     tok, width = ctx.shape
     mem = right.shape[0]
@@ -125,7 +124,7 @@
     units = width // LANES
     last = units - 1
     pieces = tok // LANES
-    upper = tok - 64
+    upper = LANES
     per = mem // 2
     members = mem * n_pop
     p = lax.axis_index("pop")
@@ -150,15 +149,23 @@
     def wait_for(ref, sem):
         pltpu.make_async_copy(ref, ref, sem).wait()
 
-    def w_copy(s, k):
+    def w_copy(s, k, sem):
         start = pl.multiple_of(blocks[s] * width + k * BLK, BLK)
-        sem = near_sem if s == 3 else w_sem.at[s, k % 3]
         return pltpu.make_async_copy(w_h.at[:, pl.ds(start, BLK)], w_v.at[s, k], sem)
 
     def w_first(n):
-        block = (other, other + 1, diagonal, across)[n]
-        start = pl.multiple_of(block * width + (n // 2) * LANES, LANES)
-        return pltpu.make_async_copy(w_h.at[:, pl.ds(start, LANES)], w_top.at[n], top_sem.at[n])
+        start = pl.multiple_of((other + n) * width, BLK)
+        slot = 1 - c if n == 0 else c
+        return pltpu.make_async_copy(w_h.at[:, pl.ds(start, BLK)], w_v.at[slot, 0], top_sem.at[n])
+
+    def near_copy(k):
+        return w_copy(3, k, near_sem)
+
+    def w_step(k, more):
+        steps = [(1, k), (2, k)] if isinstance(k, jax.Array) or k > 0 else [(2, k)]
+        if more:
+            steps.append((0, k + 1))
+        return [w_copy(s, i, w_sem.at[k % 2]) for s, i in steps]
 
     my_cols = pl.ds(pl.multiple_of(q * width, BLK), width)
     my_rows = pl.ds(pl.multiple_of(p * rows, LANES), rows)
@@ -166,16 +173,16 @@
         pltpu.make_async_copy(ctx_h.at[0:upper], ctx.at[0:upper], loc_sem.at[0]),
         pltpu.make_async_copy(ctx_h.at[upper:tok], ctx.at[upper:tok], loc_sem.at[1]),
         pltpu.make_async_copy(res_h, res, loc_sem.at[2]),
-        pltpu.make_async_copy(tgt_h, tgt, loc_sem.at[3]),
-        pltpu.make_async_copy(left_h.at[:, my_cols], lcols, loc_sem.at[4]),
-        pltpu.make_async_copy(left_h.at[:, my_rows], lall.at[0], loc_sem.at[5]),
-        pltpu.make_async_copy(right_h.at[:, my_cols], rall.at[0], loc_sem.at[6]),
-        pltpu.make_async_copy(gain_h, gain, loc_sem.at[7]),
-        pltpu.make_async_copy(right_h, right, loc_sem.at[8]),
-        pltpu.make_async_copy(ranks_h, ranks, loc_sem.at[9]),
+        pltpu.make_async_copy(tgt_h, tgt, loc_sem.at[2]),
+        pltpu.make_async_copy(left_h.at[:, my_cols], lcols, loc_sem.at[2]),
+        pltpu.make_async_copy(left_h.at[:, my_rows], lall.at[0], loc_sem.at[2]),
+        pltpu.make_async_copy(right_h.at[:, my_cols], rall.at[0], loc_sem.at[2]),
+        pltpu.make_async_copy(gain_h, gain, loc_sem.at[2]),
+        pltpu.make_async_copy(right_h, right, loc_sem.at[2]),
+        pltpu.make_async_copy(ranks_h, ranks, loc_sem.at[2]),
     ]
+    locals_[0].start()
     w_first(0).start()
-    locals_[0].start()
     locals_[1].start()
     w_first(1).start()
 
@@ -185,29 +192,28 @@
     for bit in (1, 2, 4):
         signal(barrier, flip(p, bit), q)
 
-    def copy_top():
-        return remote(first_v.at[0:upper], direct.at[c], s_top, r_top, p, other)
-
-    def copy_a(first, count, n):
-        cols = pl.ds(first, count)
-        return remote(send.at[0, cols], recv.at[0, cols], sent, r_a.at[n], p, mate)
-
-    def copy_a0(core):
-        if core == 1:
-            return remote(first_v.at[upper:tok], recv.at[0, 0, upper:tok], s_a0, r_a.at[0], p, mate)
-        return remote(send.at[0, 0], recv.at[0, 0], s_a0, r_a.at[0], p, mate)
-
-    def copy_y0(core):
-        part = slice(0 if core == 1 else upper, tok)
-        return remote(send.at[1, 0, part], recv.at[1, 0, part], s_a0, r_y.at[0], p, across)
-
-    def copy_y(first, count, n):
-        cols = pl.ds(first, count)
-        return remote(send.at[1, cols], recv.at[1, cols], sent, r_y.at[n], p, across)
+    copy_top = remote(first_v, direct.at[c], sent, r_top, p, other)
+
+    def copy_a(k):
+        cols = pl.ds(2 * k, 2)
+        return remote(send.at[0, cols], recv.at[0, cols], sent, r_a.at[pieces + k - 1], p, mate)
+
+    def strip(i):
+        return pl.ds(i * LANES, LANES)
+
+    def copy_a0(i):
+        return remote(send.at[0, 0:2, strip(i)], recv.at[0, 0:2, strip(i)], sent, r_a.at[i], p, mate)
+
+    def copy_y0(i):
+        return remote(send.at[1, 0:2, strip(i)], recv.at[1, 0:2, strip(i)], sent, r_y.at[i], p, across)
+
+    def copy_y(k, count=2):
+        cols = pl.ds(2 * k, count)
+        return remote(send.at[1, cols], recv.at[1, cols], sent, r_y.at[pieces + k - 1], p, across)
 
     def copy_end(i):
         part = slice(i * LANES, (i + 1) * LANES)
-        return remote(send.at[1, last, part], recv.at[1, last, part], sent, r_y.at[chunks + 1 + i], p, across)
+        return remote(send.at[1, last, part], recv.at[1, last, part], sent, r_y.at[pieces + chunks - 1 + i], p, across)
 
     def copy_b(k):
         cols = pl.ds(2 * k, 2)
@@ -216,20 +222,20 @@
     def copy_l(d):
         peer = flip(p, d)
         cols = pl.ds(pl.multiple_of(peer * rows, LANES), rows)
-        return remote(left_h.at[:, cols], lall.at[d], s_l, r_l, peer, q)
+        return remote(left_h.at[:, cols], lall.at[d], sent, r_l, peer, q)
 
     def copy_r(d):
-        return remote(right_h.at[:, my_cols], rall.at[d], s_r, r_r, flip(p, d), q)
+        return remote(right_h.at[:, my_cols], rall.at[d], sent, r_r, flip(p, d), q)
 
     def copy_f(n, core):
         target = flip(q, 2 * (n % 2)) - c + core
-        return remote(fits.at[0], fits.at[n], s_f.at[core], r_f, flip(p, n // 2), target)
-
-    copy_lin = remote(lin, lin_in, s_lin, r_lin, p, mate)
-    copy_far = remote(lin_out, lin_far, s_far, r_far, p, across)
+        return remote(fits.at[0], fits.at[n], sent, r_f, flip(p, n // 2), target)
+
+    copy_lin = remote(lin, lin_in, sent, r_lin, p, mate)
+    copy_far = remote(lin_out, lin_far, sent, r_far, p, across)
 
     def copy_post(i, d):
-        return remote(post.at[i], post_in.at[d - 1, i], s_post, r_post, p, flip(q, d))
+        return remote(post.at[i], post_in.at[d - 1, i], sent, r_post, p, flip(q, d))
 
     def split_store(which, k, value):
         send[which, 2 * k] = value[:, :LANES]
@@ -237,96 +243,101 @@
 
     def product(s, k):
         return jnp.dot(ctx[...], w_v[s, k], preferred_element_type=F32)
-
-    def narrow(n, part):
-        return jnp.dot(ctx[part, :], w_top[n], preferred_element_type=F32)
 
     everything = slice(0, tok)
     with jax.named_scope("load0"):
         locals_[0].wait()
         w_first(0).wait()
-    w_first(2).start()
-    w_first(3).start()
-    first_v[0:upper] = narrow(0, slice(0, upper)).astype(BF)
+    top = jnp.dot(ctx[0:upper, :], w_v[1 - c, 0], preferred_element_type=F32).astype(BF)
+    first_v[0] = top[:, :LANES]
+    first_v[1] = top[:, LANES:]
     with jax.named_scope("barrier"):
         pl.semaphore_wait(barrier, 6)
-    copy_top().start()
+    copy_top.start()
     signal(rounds.at[0], flip(p, 1), q)
+    for item in w_step(0, True):
+        item.start()
     locals_[1].wait()
     w_first(1).wait()
-    second = narrow(1, everything)
+
+    def strip_product(s, i):
+        rows_i = slice(i * LANES, (i + 1) * LANES)
+        return jnp.dot(ctx[rows_i, :], w_v[s, 0], preferred_element_type=F32)
+
+    def give(i):
+        value = strip_product(0, i).astype(BF)
+        send[0, 0, strip(i)] = value[:, :LANES]
+        send[0, 1, strip(i)] = value[:, LANES:]
+        copy_a0(i).start()
+
+    def pass_on(i, value):
+        send[1, 0, strip(i)] = (value[:, :LANES] + recv[0, 0, strip(i)].astype(F32)).astype(BF)
+        send[1, 1, strip(i)] = (value[:, LANES:] + recv[0, 1, strip(i)].astype(F32)).astype(BF)
+        copy_y0(i).start()
+
+    for i in range(1, pieces):
+        give(i)
 
     @pl.when(c == 0)
     def _():
-        send[0, 0] = second.astype(BF)
-        copy_a0(0).start()
-
-    low_rows = narrow(0, slice(upper, tok))
-    first_v[upper:tok] = low_rows.astype(BF)
+        give(0)
+        send[1, 0, strip(0)] = first_v[0]
+        send[1, 1, strip(0)] = first_v[1]
+
+    for item in w_step(1, True):
+        item.start()
+    near_copy(0).start()
+    mine = [strip_product(1, i) for i in range(1, pieces)]
+    with jax.named_scope("wait_a0"):
+        for i in range(1, pieces):
+            copy_a0(i).wait_recv()
+            pass_on(i, mine[i - 1])
 
     @pl.when(c == 1)
     def _():
-        copy_a0(1).start()
-
-    w_copy(0, 1).start()
-    w_copy(1, 1).start()
-
-    for k in (0, 1):
-        w_copy(2, k).start()
-    for s in range(3):
-        w_copy(s, 2).start()
-    w_copy(3, 0).start()
-    w_first(2).wait()
-    send[0, 1] = narrow(2, everything).astype(BF)
-    copy_a(1, 1, 1).start()
-    w_first(3).wait()
-    third = narrow(3, everything)
-
-    with jax.named_scope("wait_a0"):
-        @pl.when(c == 0)
-        def _():
-            copy_a0(1).wait_recv()
-            send[1, 0, 0:upper] = first_v[0:upper]
-            send[1, 0, upper:tok] = (low_rows + recv[0, 0, upper:tok].astype(F32)).astype(BF)
-            copy_y0(0).start()
-
-        @pl.when(c == 1)
-        def _():
-            copy_a0(0).wait_recv()
-            send[1, 0] = (second + recv[0, 0].astype(F32)).astype(BF)
-            copy_y0(1).start()
-
-    w_copy(0, 1).wait()
+        value = strip_product(1, 0)
+        copy_a0(0).wait_recv()
+        pass_on(0, value)
+
+    for item in w_step(0, True):
+        item.wait()
     split_store(0, 1, product(0, 1).astype(BF))
-    copy_a(2, 2, 2).start()
-    with jax.named_scope("wait_a1"):
-        copy_a(1, 1, 1).wait_recv()
-    send[1, 1] = (third + recv[0, 1].astype(F32)).astype(BF)
-    copy_y(1, 1, 1).start()
-    w_copy(2, 0).wait()
+    copy_a(1).start()
+    for item in w_step(2, True):
+        item.start()
 
     def far(k, carry):
-        w_copy(1, k).wait()
+        for item in w_step(k, False):
+            item.wait()
+
+        @pl.when(k + 1 < chunks)
+        def _():
+            w_copy(0, k + 1, w_sem.at[k % 2]).wait()
+
         mine = product(1, k)
         with jax.named_scope("wait_a"):
-            copy_a(2 * k, 2, k + 1).wait_recv()
+            copy_a(k).wait_recv()
         send[1, 2 * k] = (mine[:, :LANES] + recv[0, 2 * k].astype(F32)).astype(BF)
         send[1, 2 * k + 1] = (mine[:, LANES:] + recv[0, 2 * k + 1].astype(F32)).astype(BF)
 
         @pl.when(k + 1 < chunks)
         def _():
-            copy_y(2 * k, 2, k + 1).start()
+            copy_y(k).start()
 
         @pl.when(k + 1 == chunks)
         def _():
-            copy_y(2 * k, 1, k + 1).start()
+            copy_y(k, 1).start()
 
         @pl.when(k + 2 < chunks)
         def _():
-            for s in range(3):
-                w_copy(s, k + 2).start()
-
-        w_copy(3, k).start()
+            for item in w_step(k + 2, False):
+                item.start()
+
+        @pl.when(k + 3 < chunks)
+        def _():
+            w_copy(0, k + 3, w_sem.at[k % 2]).start()
+
+        near_copy(k).start()
 
         @pl.when(k == 1)
         def _():
@@ -349,16 +360,14 @@
 
         @pl.when(k + 1 < chunks)
         def _():
-            w_copy(0, k + 1).wait()
             split_store(0, k + 1, product(0, k + 1).astype(BF))
-            copy_a(2 * k + 2, 2, k + 2).start()
+            copy_a(k + 1).start()
 
         @pl.when(k == 1)
         def _():
             split_store(2, 0, product(2, 0).astype(BF))
             copy_b(0).start()
 
-        w_copy(2, k).wait()
         split_store(2, k, product(2, k).astype(BF))
         copy_b(k).start()
         return carry
@@ -422,7 +431,9 @@
     with jax.named_scope("wait_b"):
         wait_for(recv.at[2], r_b)
     with jax.named_scope("linear"):
-        top = nt_dot(mixed(other, 0, LANES), first_v[0:upper]) * jnp.where(c == 1, 1.0, 0.0)
+        top_rows = mixed(other, 0, BLK)
+        top = nt_dot(top_rows[:, :LANES], first_v[0]) + nt_dot(top_rows[:, LANES:], first_v[1])
+        top = top * jnp.where(c == 1, 1.0, 0.0)
         top = jnp.concatenate([top, jnp.zeros((3 * mem, tok - upper), F32)], axis=1)
         carry = (top[0:mem], top[mem:2 * mem] + top[2 * mem:3 * mem])
         crossed, crossed_g = lax.fori_loop(0, chunks, linear, carry)
@@ -449,20 +460,21 @@
         return carry
 
     with jax.named_scope("wait_y0"):
+        for i in range(1, pieces):
+            copy_y0(i).wait_recv()
+
         @pl.when(c == 0)
         def _():
             wait_for(direct, r_top)
+            for u in range(2):
+                recv[1, u, strip(0)] = jnp.zeros((upper, LANES), BF)
+                base[0:upper, u * LANES:(u + 1) * LANES] += direct[0, u].astype(F32) + direct[1, u].astype(F32)
+
+        @pl.when(c == 1)
+        def _():
             copy_y0(0).wait_recv()
-            recv[1, 0, 0:upper] = jnp.zeros((upper, LANES), BF)
-            base[0:upper, 0:LANES] += direct[0].astype(F32) + direct[1].astype(F32)
-
-        @pl.when(c == 1)
-        def _():
-            copy_y0(1).wait_recv()
-
-    settle(0, 0)
-    copy_y(1, 1, 1).wait_recv()
-    settle(1, 0)
+
+    lax.fori_loop(0, 2, settle, 0)
 
     @pl.when(c == 1)
     def _():
@@ -475,7 +487,7 @@
 
     def settle_chunk(k, carry):
         with jax.named_scope("wait_y"):
-            copy_y(2 * k, 2, k + 1).wait_recv()
+            copy_y(k).wait_recv()
         settle(2 * k, 0)
         settle(2 * k + 1, 0)
         return carry
@@ -483,7 +495,7 @@
     with jax.named_scope("settle"):
         lax.fori_loop(1, chunks - 1, settle_chunk, 0)
     with jax.named_scope("wait_y8"):
-        copy_y(last - 1, 1, chunks).wait_recv()
+        copy_y(chunks - 1, 1).wait_recv()
     settle(last - 1, 0)
     before = nt_dot(row_picker(4), halves((sq_s[...], sq_a[...], sq_e[...], sq_t[...])))
     lane = lax.broadcasted_iota(jnp.int32, (1, mem), 1)
@@ -550,33 +562,16 @@
         wait_for(rall.at[half_of], r_r)
     for d in range(n_pop):
         right_all[d * mem:(d + 1) * mem, :] = rall[d]
-    with jax.named_scope("drain"):
-        for which in range(3):
-            wait_for(send.at[which, 1:units], sent)
-        wait_for(send.at[2, 0], sent)
-        wait_for(first_v.at[0:upper], s_top)
-        wait_for(lall.at[half_of], s_l)
-        wait_for(rall.at[half_of], s_r)
-
-        @pl.when(c == 0)
-        def _():
-            copy_a0(0).wait_send()
-            copy_y0(0).wait_send()
-            copy_lin.wait_send()
-            wait_for(post_in.at[0:2], s_post)
-            with jax.named_scope("wait_f"):
-                wait_for(fits, r_f)
-
-        @pl.when(c == 1)
-        def _():
-            copy_a0(1).wait_send()
-            copy_y0(1).wait_send()
-            copy_far.wait_send()
-            wait_for(post_in.at[0], s_post)
-            with jax.named_scope("wait_f"):
-                wait_for(others, r_f)
-            wait_for(fits, s_f.at[0])
-            wait_for(others, s_f.at[1])
+
+    @pl.when(c == 0)
+    def _():
+        with jax.named_scope("wait_f"):
+            wait_for(fits, r_f)
+
+    @pl.when(c == 1)
+    def _():
+        with jax.named_scope("wait_f"):
+            wait_for(others, r_f)
 
     with jax.named_scope("weights"):
         rows_of = [fits[2 * d] + fits[2 * d + 1] for d in range(n_pop)]
@@ -590,6 +585,28 @@
         for d in range(n_pop):
             upright = jnp.sum(jnp.where(eye, weight[d:d + 1], 0.0), axis=1, keepdims=True)
             weighted[d * mem:(d + 1) * mem, :] = (upright * lall[d].astype(F32)).astype(BF)
+
+    for which in range(2):
+        wait_for(send.at[which, 2:units], sent)
+    wait_for(send.at[2], sent)
+    wait_for(first_v, sent)
+    wait_for(lall.at[half_of], sent)
+    wait_for(rall.at[half_of], sent)
+    for core in range(2):
+        @pl.when(c == core)
+        def _(core=core):
+            for i in range(core, pieces):
+                copy_a0(i).wait_send()
+            for i in range(1 - core, pieces):
+                copy_y0(i).wait_send()
+            if core == 0:
+                copy_lin.wait_send()
+                wait_for(post_in.at[0:2], sent)
+            else:
+                copy_far.wait_send()
+                wait_for(post_in.at[0], sent)
+                wait_for(fits, sent)
+                wait_for(others, sent)
 
 
 def in_hbm(x):
@@ -625,7 +642,6 @@
         out_specs=[vmem] * 4,
         scratch_shapes=[
             pltpu.VMEM((4, chunks, width, BLK), BF),
-            pltpu.VMEM((4, width, LANES), BF),
             pltpu.VMEM((tok, width), BF),
             pltpu.VMEM((tok, width), BF),
             pltpu.VMEM((tok, width), BF),
@@ -635,8 +651,8 @@
             pltpu.VMEM((1, mem), jnp.int32),
             pltpu.VMEM((3, units, tok, LANES), BF),
             pltpu.VMEM((3, units, tok, LANES), BF),
-            pltpu.VMEM((tok, LANES), BF),
-            pltpu.VMEM((2, tok - 64, LANES), BF),
+            pltpu.VMEM((2, LANES, LANES), BF),
+            pltpu.VMEM((2, 2, LANES, LANES), BF),
             pltpu.VMEM((n_pop, mem, rows), BF),
             pltpu.VMEM((n_pop, mem, width), BF),
             acc, acc, acc, acc,
@@ -647,16 +663,15 @@
             pltpu.VMEM((pieces, 4, LANES), F32),
             pltpu.VMEM((n_mp - 1, pieces, 4, LANES), F32),
             pltpu.VMEM((2 * n_pop, 2, mem), F32),
-            dma((3, 3)),
-            dma((4,)),
+            dma((2,)),
+            dma((2,)),
             dma,
-            dma((10,)),
+            dma((3,)),
             dma,
-            dma((chunks + 1,)),
-            dma((chunks + 1 + pieces,)),
+            dma((chunks - 1 + pieces,)),
+            dma((chunks - 1 + 2 * pieces,)),
         ]
-        + [dma] * 14
-        + [dma((2,)), dma]
+        + [dma] * 8
         + [pltpu.SemaphoreType.REGULAR((3,))],
         compiler_params=pltpu.CompilerParams(
             collective_id=0, has_side_effects=True, vmem_limit_bytes=48 * 1024 * 1024

time: 41.1 us -> 39.6 us (0.964)
  Pallas kernels: 40.3 us -> 38.8 us
    pallas_call x1, Pallas kernels: 37.9 us -> 36.3 us  [fused_shards(): pl.pallas_call(functools.partial(kernel, n_pop, n_mp), name='es_step', ou...]
where the time goes in v3:
time: 39.6 us; the launch traced here: 39.4 us
  Pallas kernels  38.8 us (98%)
  between operations  0.64 us (2%)
    pallas_call x1, Pallas kernels, fused_shards(): pl.pallas_call(functools.partial(kernel, n_pop, n_mp), name='es_step', ou...  36.3 us
    pallas_call x1, Pallas kernels, fused_shards(): pl.pallas_call(functools.partial(finish, math.sqrt(count_all) / SIGMA), n...  2.43 us

profile of v3, /device:TPU:0, one launch (start us, length us, event | category | flops | bytes accessed | tf_op | source)
XLA Modules:
  0.0 39.4 jit_solution(3564186814482900991)
XLA Ops:
  0.6 36.3 %es_step.1 = (f32[384,1280]{1,0:T(8,128)S(1)}, bf16[128,640]{1,0:T(8,128)(2,1)S(1)}, bf16[128,1280]{1,0:T(8,128)(2,1)S(1)}, f32[1,16]{1,0:T(1,128)S(1)}) custom-call(bf16[384,1280]{1,0:T(8,128)(2,1)} %ctx_h.1, bf16[1280,5120]{1,0:T(8,128)(2,1)} %w_h.1, bf16[384,1280]{1,0:T(8,128)(2,1)} %res_h.1, bf16[384,1280]{1,0:T(8,128)(2,1)} %tgt_h.1, ...), custom_call_target="tpu_custom_call" | custom-call | tf_op jit(solution)/shard_map/es_step/pallas_call | solution.py:632
  37.0 2.4 %es_update.1 = (f32[640,1280]{1,0:T(8,128)}, f32[384,1280]{1,0:T(8,128)}, f32[1,16]{1,0:T(1,128)}) custom-call(bf16[128,640]{1,0:T(8,128)(2,1)S(1)} %get-tuple-element.10.weighted, bf16[128,1280]{1,0:T(8,128)(2,1)S(1)} %get-tuple-element.11.right_all, f32[384,1280]{1,0:T(8,128)S(1)} %get-tuple-element.12.base_in, f32[1,16]{1,0:T(1,128)S(1)} %get-tuple-element.13.fit_in), custom_call_target="tpu_custom_call" | custom-call | tf_op jit(solution)/shard_map/es_update/pallas_call | solution.py:686

commit v4 on v3

--- a/solution.py
+++ b/solution.py
@@ -111,10 +111,10 @@
 
 def kernel(
     n_pop, n_mp, ctx_h, w_h, res_h, tgt_h, gain_h, left_h, right_h, ranks_h,
-    base, weighted, right_all, fit_out,
+    base, left_all, right_all, fits,
     w_v, ctx, res, tgt, lcols, gain, right, ranks, send, recv, first_v, direct, lall, rall,
-    sq_s, sq_a, sq_e, sq_t, lin, lin_in, lin_out, lin_far, post, post_in, fits,
-    w_sem, top_sem, near_sem, loc_sem, sent, r_a, r_y, r_b, r_top, r_lin, r_far, r_post, r_l, r_r, r_f, rounds,
+    sq_s, sq_a, sq_e, sq_t, lin, lin_in, lin_out, lin_far, post, post_in, swap, swap_in, marks,
+    w_sem, top_sem, near_sem, loc_sem, sent, r_a, r_y, r_b, r_top, r_lin, r_far, r_post, r_swap, r_l, r_r, r_f, rounds,
 ):
     tok, width = ctx.shape
     mem = right.shape[0]
@@ -183,12 +183,11 @@
     ]
     locals_[0].start()
     w_first(0).start()
-    locals_[1].start()
-    w_first(1).start()
 
     barrier = pltpu.get_barrier_semaphore()
     for peer in (mate, across, diagonal):
         signal(barrier, p, peer)
+    locals_[1].start()
     for bit in (1, 2, 4):
         signal(barrier, flip(p, bit), q)
 
@@ -214,6 +213,9 @@
     def copy_end(i):
         part = slice(i * LANES, (i + 1) * LANES)
         return remote(send.at[1, last, part], recv.at[1, last, part], sent, r_y.at[pieces + chunks - 1 + i], p, across)
+
+    copy_swap = remote(send.at[1, last, strip(0)], swap_in, sent, r_swap, p, mate)
+    copy_swapped = remote(swap, recv.at[1, last, strip(0)], sent, r_y.at[pieces + chunks - 1], p, diagonal)
 
     def copy_b(k):
         cols = pl.ds(2 * k, 2)
@@ -229,7 +231,7 @@
 
     def copy_f(n, core):
         target = flip(q, 2 * (n % 2)) - c + core
-        return remote(fits.at[0], fits.at[n], sent, r_f, flip(p, n // 2), target)
+        return remote(marks.at[0], marks.at[n], sent, r_f, flip(p, n // 2), target)
 
     copy_lin = remote(lin, lin_in, sent, r_lin, p, mate)
     copy_far = remote(lin_out, lin_far, sent, r_far, p, across)
@@ -248,6 +250,7 @@
     with jax.named_scope("load0"):
         locals_[0].wait()
         w_first(0).wait()
+    w_first(1).start()
     top = jnp.dot(ctx[0:upper, :], w_v[1 - c, 0], preferred_element_type=F32).astype(BF)
     first_v[0] = top[:, :LANES]
     first_v[1] = top[:, LANES:]
@@ -258,7 +261,6 @@
     for item in w_step(0, True):
         item.start()
     locals_[1].wait()
-    w_first(1).wait()
 
     def strip_product(s, i):
         rows_i = slice(i * LANES, (i + 1) * LANES)
@@ -275,30 +277,31 @@
         send[1, 1, strip(i)] = (value[:, LANES:] + recv[0, 1, strip(i)].astype(F32)).astype(BF)
         copy_y0(i).start()
 
-    for i in range(1, pieces):
-        give(i)
-
     @pl.when(c == 0)
     def _():
+        mine = [strip_product(1, i) for i in (1, 2)]
+        copy_a0(1).wait_recv()
+        pass_on(1, mine[0])
+        w_first(1).wait()
+        give(1)
+        copy_a0(2).wait_recv()
+        pass_on(2, mine[1])
+        give(2)
         give(0)
         send[1, 0, strip(0)] = first_v[0]
         send[1, 1, strip(0)] = first_v[1]
 
+    @pl.when(c == 1)
+    def _():
+        give(1)
+        give(2)
+        send[0, 0, strip(0)] = first_v[0]
+        send[0, 1, strip(0)] = first_v[1]
+        w_first(1).wait()
+
     for item in w_step(1, True):
         item.start()
     near_copy(0).start()
-    mine = [strip_product(1, i) for i in range(1, pieces)]
-    with jax.named_scope("wait_a0"):
-        for i in range(1, pieces):
-            copy_a0(i).wait_recv()
-            pass_on(i, mine[i - 1])
-
-    @pl.when(c == 1)
-    def _():
-        value = strip_product(1, 0)
-        copy_a0(0).wait_recv()
-        pass_on(0, value)
-
     for item in w_step(0, True):
         item.wait()
     split_store(0, 1, product(0, 1).astype(BF))
@@ -306,6 +309,15 @@
     for item in w_step(2, True):
         item.start()
 
+    @pl.when(c == 1)
+    def _():
+        mine = [strip_product(1, i) for i in (1, 2, 0)]
+        with jax.named_scope("wait_a0"):
+            for i in (1, 2, 0):
+                copy_a0(i).wait_recv()
+                pass_on(i, mine[i - 1])
+
+
     def far(k, carry):
         for item in w_step(k, False):
             item.wait()
@@ -327,6 +339,11 @@
         @pl.when(k + 1 == chunks)
         def _():
             copy_y(k, 1).start()
+
+            @pl.when(c == 0)
+            def _():
+                send[1, last, strip(0)] = mine[0:LANES, LANES:].astype(BF)
+                copy_swap.start()
 
         @pl.when(k + 2 < chunks)
         def _():
@@ -433,6 +450,7 @@
     with jax.named_scope("linear"):
         top_rows = mixed(other, 0, BLK)
         top = nt_dot(top_rows[:, :LANES], first_v[0]) + nt_dot(top_rows[:, LANES:], first_v[1])
+        top = top + nt_dot(mixed(other, last * LANES, LANES), send[0, last, strip(0)])
         top = top * jnp.where(c == 1, 1.0, 0.0)
         top = jnp.concatenate([top, jnp.zeros((3 * mem, tok - upper), F32)], axis=1)
         carry = (top[0:mem], top[mem:2 * mem] + top[2 * mem:3 * mem])
@@ -443,7 +461,7 @@
     @pl.when(c == 0)
     def _():
         copy_lin.start()
-        for i in range(pieces):
+        for i in range(1, pieces):
             copy_end(i).start()
 
     def arrived(u, part):
@@ -480,6 +498,9 @@
     def _():
         with jax.named_scope("wait_lin"):
             copy_lin.wait_recv()
+        copy_swap.wait_recv()
+        swap[...] = (send[0, last, strip(0)].astype(F32) + swap_in[...].astype(F32)).astype(BF)
+        copy_swapped.start()
         lin_out[...] = lin[1 - y] + lin_in[1 - y]
         copy_far.start()
         for i in range(pieces):
@@ -523,7 +544,7 @@
     square = (mem, mem)
     eye = lax.broadcasted_iota(jnp.int32, square, 0) == lax.broadcasted_iota(jnp.int32, square, 1)
     half_of = slice(1, n_pop)
-    others = fits.at[pl.ds(1, 2 * n_pop - 1)]
+    others = marks.at[pl.ds(1, 2 * n_pop - 1)]
 
     @pl.when(c == 1)
     def _():
@@ -550,8 +571,8 @@
             summed = jnp.sum(errors, axis=1, keepdims=True)
             stacked = jnp.concatenate([summed, summed], axis=0)
             total_row = jnp.sum(jnp.where(eye, stacked, 0.0), axis=0, keepdims=True)
-            fits[0, 0:1] = jnp.where(mine_lane, total_row, 0.0)
-            fits[0, 1:2] = jnp.where(mine_lane, shaped, 0.0)
+            marks[0, 0:1] = jnp.where(mine_lane, total_row, 0.0)
+            marks[0, 1:2] = jnp.where(mine_lane, shaped, 0.0)
             for n in range(2 * n_pop - 1, -1, -1):
                 copy_f(n, 0).start()
                 if n > 0:
@@ -562,30 +583,19 @@
         wait_for(rall.at[half_of], r_r)
     for d in range(n_pop):
         right_all[d * mem:(d + 1) * mem, :] = rall[d]
+        left_all[d * mem:(d + 1) * mem, :] = lall[d]
 
     @pl.when(c == 0)
     def _():
         with jax.named_scope("wait_f"):
-            wait_for(fits, r_f)
+            wait_for(marks, r_f)
 
     @pl.when(c == 1)
     def _():
         with jax.named_scope("wait_f"):
             wait_for(others, r_f)
 
-    with jax.named_scope("weights"):
-        rows_of = [fits[2 * d] + fits[2 * d + 1] for d in range(n_pop)]
-        all_fit = jnp.concatenate([row[0:1] for row in rows_of], axis=0) * (-1.0 / (tok * full))
-        all_shaped = jnp.concatenate([row[1:2] for row in rows_of], axis=0)
-        fit_out[...] = all_fit[0:1]
-        average = jnp.sum(jnp.sum(all_fit, axis=0, keepdims=True), axis=1, keepdims=True) / members
-        centre = all_fit - average
-        deviation = jnp.sqrt(jnp.sum(jnp.sum(centre * centre, axis=0, keepdims=True), axis=1, keepdims=True) / members + 1e-05)
-        weight = all_shaped + centre / deviation / members
-        for d in range(n_pop):
-            upright = jnp.sum(jnp.where(eye, weight[d:d + 1], 0.0), axis=1, keepdims=True)
-            weighted[d * mem:(d + 1) * mem, :] = (upright * lall[d].astype(F32)).astype(BF)
-
+    fits[...] = marks[...]
     for which in range(2):
         wait_for(send.at[which, 2:units], sent)
     wait_for(send.at[2], sent)
@@ -599,13 +609,15 @@
                 copy_a0(i).wait_send()
             for i in range(1 - core, pieces):
                 copy_y0(i).wait_send()
+            if core == 1:
+                copy_swapped.wait_send()
             if core == 0:
                 copy_lin.wait_send()
                 wait_for(post_in.at[0:2], sent)
             else:
                 copy_far.wait_send()
                 wait_for(post_in.at[0], sent)
-                wait_for(fits, sent)
+                wait_for(marks, sent)
                 wait_for(others, sent)
 
 
@@ -629,14 +641,14 @@
     dma = pltpu.SemaphoreType.DMA
     acc = pltpu.VMEM((tok, LANES), F32)
     group = (2 * mem, tok)
-    base, weighted, right_all, fitness = pl.pallas_call(
+    base, left_all, right_all, fits = pl.pallas_call(
         functools.partial(kernel, n_pop, n_mp),
         name="es_step",
         out_shape=(
             jax.ShapeDtypeStruct((tok, width), F32),
             jax.ShapeDtypeStruct((n_pop * mem, rows), BF),
             jax.ShapeDtypeStruct((n_pop * mem, width), BF),
-            jax.ShapeDtypeStruct((1, mem), F32),
+            jax.ShapeDtypeStruct((2 * n_pop, 2, mem), F32),
         ),
         in_specs=[anywhere] * 8,
         out_specs=[vmem] * 4,
@@ -662,6 +674,8 @@
             pltpu.VMEM(group, F32),
             pltpu.VMEM((pieces, 4, LANES), F32),
             pltpu.VMEM((n_mp - 1, pieces, 4, LANES), F32),
+            pltpu.VMEM((LANES, LANES), BF),
+            pltpu.VMEM((LANES, LANES), BF),
             pltpu.VMEM((2 * n_pop, 2, mem), F32),
             dma((2,)),
             dma((2,)),
@@ -671,7 +685,7 @@
             dma((chunks - 1 + pieces,)),
             dma((chunks - 1 + 2 * pieces,)),
         ]
-        + [dma] * 8
+        + [dma] * 9
         + [pltpu.SemaphoreType.REGULAR((3,))],
         compiler_params=pltpu.CompilerParams(
             collective_id=0, has_side_effects=True, vmem_limit_bytes=48 * 1024 * 1024
@@ -684,7 +698,7 @@
     )
     count_all = n_pop * mem
     update, base, fitness = pl.pallas_call(
-        functools.partial(finish, math.sqrt(count_all) / SIGMA),
+        functools.partial(finish, math.sqrt(count_all) / SIGMA, tok * full),
         name="es_update",
         out_shape=(
             jax.ShapeDtypeStruct((rows, width), F32),
@@ -693,20 +707,42 @@
         ),
         in_specs=[vmem] * 4,
         out_specs=[anywhere] * 3,
-        scratch_shapes=[pltpu.VMEM((rows, width), F32), dma((rows // 128 + 2,))],
+        scratch_shapes=[
+            pltpu.VMEM((rows, width), F32),
+            pltpu.VMEM((n_pop * mem, rows), BF),
+            pltpu.VMEM((1, mem), F32),
+            dma((rows // 128 + 2,)),
+        ],
         compiler_params=pltpu.CompilerParams(vmem_limit_bytes=16 * 1024 * 1024),
-    )(weighted, right_all, base, fitness)
+    )(left_all, right_all, base, fits)
     return (update, fitness.reshape(mem), base)
 
 
-def finish(scale, weighted, right_all, base_in, fit_in, update, base, fit, held, sems):
+def finish(scale, count, left_all, right_all, base_in, fits, update, base, fit, held, weighted, fit_v, sems):
     steps = held.shape[0] // 128
+    mem = fit_v.shape[1]
+    n_pop = left_all.shape[0] // mem
+    members = n_pop * mem
     copies = [
         pltpu.make_async_copy(base_in, base, sems.at[steps]),
-        pltpu.make_async_copy(fit_in, fit, sems.at[steps + 1]),
+        pltpu.make_async_copy(fit_v, fit, sems.at[steps + 1]),
     ]
     copies[0].start()
+    rows_of = [fits[2 * d] + fits[2 * d + 1] for d in range(n_pop)]
+    all_fit = jnp.concatenate([row[0:1] for row in rows_of], axis=0) * (-1.0 / count)
+    all_shaped = jnp.concatenate([row[1:2] for row in rows_of], axis=0)
+    fit_v[...] = all_fit[0:1]
     copies[1].start()
+    average = jnp.sum(jnp.sum(all_fit, axis=0, keepdims=True), axis=1, keepdims=True) / members
+    centre = all_fit - average
+    deviation = jnp.sqrt(jnp.sum(jnp.sum(centre * centre, axis=0, keepdims=True), axis=1, keepdims=True) / members + 1e-05)
+    weight = all_shaped + centre / deviation / members
+    square = (mem, mem)
+    eye = lax.broadcasted_iota(jnp.int32, square, 0) == lax.broadcasted_iota(jnp.int32, square, 1)
+    for d in range(n_pop):
+        part = slice(d * mem, (d + 1) * mem)
+        upright = jnp.sum(jnp.where(eye, weight[d:d + 1], 0.0), axis=1, keepdims=True)
+        weighted[part, :] = (upright * left_all[part, :].astype(F32)).astype(BF)
     for i in range(steps):
         part = slice(i * 128, (i + 1) * 128)
         held[part, :] = lax.dot_general(

time: 39.6 us -> 39.4 us (level)
    pallas_call x1, Pallas kernels: 36.3 us -> 35.9 us  [fused_shards(): pl.pallas_call(functools.partial(kernel, n_pop, n_mp), name='es_step', ou...]
where the time goes in v4:
time: 39.4 us; the launch traced here: 39.2 us
  Pallas kernels  38.5 us (98%)
  between operations  0.64 us (2%)
    pallas_call x1, Pallas kernels, fused_shards(): pl.pallas_call(functools.partial(kernel, n_pop, n_mp), name='es_step', ou...  35.9 us
    pallas_call x1, Pallas kernels, fused_shards(): pl.pallas_call(functools.partial(finish, math.sqrt(count_all) / SIGMA, to...  2.62 us

profile of v4, /device:TPU:0, one launch (start us, length us, event | category | flops | bytes accessed | tf_op | source)
XLA Modules:
  0.0 39.2 jit_solution(11315493942488180207)
XLA Ops:
  0.6 35.9 %es_step.1 = (f32[384,1280]{1,0:T(8,128)S(1)}, bf16[128,640]{1,0:T(8,128)(2,1)S(1)}, bf16[128,1280]{1,0:T(8,128)(2,1)S(1)}, f32[16,2,16]{2,1,0:T(2,128)S(1)}) custom-call(bf16[384,1280]{1,0:T(8,128)(2,1)} %ctx_h.1, bf16[1280,5120]{1,0:T(8,128)(2,1)} %w_h.1, bf16[384,1280]{1,0:T(8,128)(2,1)} %res_h.1, bf16[384,1280]{1,0:T(8,128)(2,1)} %tgt_h.1, ...), custom_call_target="tpu_custom_call" | custom-call | tf_op jit(solution)/shard_map/es_step/pallas_call | solution.py:644
  36.6 2.6 %es_update.1 = (f32[640,1280]{1,0:T(8,128)}, f32[384,1280]{1,0:T(8,128)}, f32[1,16]{1,0:T(1,128)}) custom-call(bf16[128,640]{1,0:T(8,128)(2,1)S(1)} %get-tuple-element.10.left_all, bf16[128,1280]{1,0:T(8,128)(2,1)S(1)} %get-tuple-element.11.right_all, f32[384,1280]{1,0:T(8,128)S(1)} %get-tuple-element.12.base_in, f32[16,2,16]{2,1,0:T(2,128)S(1)} %get-tuple-element.13.fits), custom_call_target="tpu_custom_call" | custom-call | tf_op jit(solution)/shard_map/es_update/pallas_call | solution.py:700

commit v5 on v4

--- a/solution.py
+++ b/solution.py
@@ -111,10 +111,10 @@
 
 def kernel(
     n_pop, n_mp, ctx_h, w_h, res_h, tgt_h, gain_h, left_h, right_h, ranks_h,
-    base, left_all, right_all, fits,
+    base, left_t, right_all, fits,
     w_v, ctx, res, tgt, lcols, gain, right, ranks, send, recv, first_v, direct, lall, rall,
-    sq_s, sq_a, sq_e, sq_t, lin, lin_in, lin_out, lin_far, post, post_in, swap, swap_in, marks,
-    w_sem, top_sem, near_sem, loc_sem, sent, r_a, r_y, r_b, r_top, r_lin, r_far, r_post, r_swap, r_l, r_r, r_f, rounds,
+    sq_s, sq_a, sq_e, sq_t, lin, lin_in, lin_out, lin_far, post, post_in, swap, swap_in, marks, left_v, ranked,
+    w_sem, top_sem, near_sem, loc_sem, sent, r_a, r_y, r_b, r_top, r_lin, r_far, r_post, r_swap, r_l, r_r, r_u, r_f, rounds,
 ):
     tok, width = ctx.shape
     mem = right.shape[0]
@@ -229,6 +229,9 @@
     def copy_r(d):
         return remote(right_h.at[:, my_cols], rall.at[d], sent, r_r, flip(p, d), q)
 
+    def copy_u(d):
+        return remote(ranked.at[0], ranked.at[d], sent, r_u, flip(p, d), q)
+
     def copy_f(n, core):
         target = flip(q, 2 * (n % 2)) - c + core
         return remote(marks.at[0], marks.at[n], sent, r_f, flip(p, n // 2), target)
@@ -247,6 +250,7 @@
         return jnp.dot(ctx[...], w_v[s, k], preferred_element_type=F32)
 
     everything = slice(0, tok)
+    order = [*range(1, pieces), 0]
     with jax.named_scope("load0"):
         locals_[0].wait()
         w_first(0).wait()
@@ -336,14 +340,10 @@
         def _():
             copy_y(k).start()
 
-        @pl.when(k + 1 == chunks)
-        def _():
-            copy_y(k, 1).start()
-
-            @pl.when(c == 0)
-            def _():
-                send[1, last, strip(0)] = mine[0:LANES, LANES:].astype(BF)
-                copy_swap.start()
+        @pl.when((k + 1 == chunks) & (c == 0))
+        def _():
+            send[1, last, strip(0)] = mine[0:LANES, LANES:].astype(BF)
+            copy_swap.start()
 
         @pl.when(k + 2 < chunks)
         def _():
@@ -396,6 +396,14 @@
         item.wait()
     wait_for(w_v.at[3], near_sem)
 
+    lane = lax.broadcasted_iota(jnp.int32, (1, LANES), 1)
+    ceiling = math.log(members / 2 + 1)
+    whole = sum(max(0.0, ceiling - math.log(i + 1.0)) for i in range(members))
+    shaped = jnp.maximum(0.0, ceiling - jnp.log(ranks[...].astype(F32) + 1.0)) / whole - 1.0 / members
+    ranked[0] = jnp.where(lane // mem == p, jnp.concatenate([shaped] * n_pop, axis=1), 0.0)
+    for d in range(1, n_pop):
+        copy_u(d).start()
+
     def near(k, carry):
         cols = pl.ds(pl.multiple_of(k * BLK, BLK), BLK)
         base[:, cols] = product(3, k) + res[:, cols].astype(F32)
@@ -403,6 +411,14 @@
 
     with jax.named_scope("near"):
         lax.fori_loop(0, chunks, near, 0)
+
+    @pl.when(c == 1)
+    def _():
+        copy_swap.wait_recv()
+        swap[...] = (send[0, last, strip(0)].astype(F32) + swap_in[...].astype(F32)).astype(BF)
+        copy_swapped.start()
+
+    copy_y(chunks - 1, 1).start()
 
     def spread(slot, value):
         for j in range(2):
@@ -461,7 +477,7 @@
     @pl.when(c == 0)
     def _():
         copy_lin.start()
-        for i in range(1, pieces):
+        for i in order[:-1]:
             copy_end(i).start()
 
     def arrived(u, part):
@@ -496,15 +512,12 @@
 
     @pl.when(c == 1)
     def _():
+        for i in order:
+            copy_end(i).start()
         with jax.named_scope("wait_lin"):
             copy_lin.wait_recv()
-        copy_swap.wait_recv()
-        swap[...] = (send[0, last, strip(0)].astype(F32) + swap_in[...].astype(F32)).astype(BF)
-        copy_swapped.start()
         lin_out[...] = lin[1 - y] + lin_in[1 - y]
         copy_far.start()
-        for i in range(pieces):
-            copy_end(i).start()
 
     def settle_chunk(k, carry):
         with jax.named_scope("wait_y"):
@@ -515,17 +528,23 @@
 
     with jax.named_scope("settle"):
         lax.fori_loop(1, chunks - 1, settle_chunk, 0)
+    half_of = slice(1, n_pop)
+    with jax.named_scope("wait_lr"):
+        wait_for(lall.at[half_of], r_l)
+        wait_for(rall.at[half_of], r_r)
+        wait_for(ranked.at[half_of], r_u)
+    with jax.named_scope("turn"):
+        for d in range(n_pop):
+            place = pl.ds(pl.multiple_of(flip(p, d) * mem, mem), mem)
+            right_all[place, :] = rall[d]
+            left_v[place, :] = lall[d].astype(F32)
+        left_t[...] = left_v[...].T
     with jax.named_scope("wait_y8"):
         copy_y(chunks - 1, 1).wait_recv()
     settle(last - 1, 0)
     before = nt_dot(row_picker(4), halves((sq_s[...], sq_a[...], sq_e[...], sq_t[...])))
-    lane = lax.broadcasted_iota(jnp.int32, (1, mem), 1)
-    mine_lane = lane // per == y
-    ceiling = math.log(members / 2 + 1)
-    whole = sum(max(0.0, ceiling - math.log(i + 1.0)) for i in range(members))
-    shaped = jnp.maximum(0.0, ceiling - jnp.log(ranks[...].astype(F32) + 1.0)) / whole - 1.0 / members
     picker = row_picker(3)
-    for i in range(pieces):
+    for i in order:
         part = slice(i * LANES, (i + 1) * LANES)
         with jax.named_scope("wait_end"):
             copy_end(i).wait_recv()
@@ -541,9 +560,6 @@
             def _():
                 copy_post(i, 2).start()
 
-    square = (mem, mem)
-    eye = lax.broadcasted_iota(jnp.int32, square, 0) == lax.broadcasted_iota(jnp.int32, square, 1)
-    half_of = slice(1, n_pop)
     others = marks.at[pl.ds(1, 2 * n_pop - 1)]
 
     @pl.when(c == 1)
@@ -569,22 +585,14 @@
             inverse = lax.rsqrt(meansq + EPSILON)
             errors = inverse * inverse * (late[1:2] + extra_a) - 2.0 * inverse * (late[2:3] + extra_e) + late[3:4]
             summed = jnp.sum(errors, axis=1, keepdims=True)
-            stacked = jnp.concatenate([summed, summed], axis=0)
-            total_row = jnp.sum(jnp.where(eye, stacked, 0.0), axis=0, keepdims=True)
-            marks[0, 0:1] = jnp.where(mine_lane, total_row, 0.0)
-            marks[0, 1:2] = jnp.where(mine_lane, shaped, 0.0)
+            spot = lax.broadcasted_iota(jnp.int32, (per, LANES), 0) + (p * mem + y * per)
+            here = lax.broadcasted_iota(jnp.int32, (per, LANES), 1) == spot
+            marks[0] = jnp.sum(jnp.where(here, summed, 0.0), axis=0, keepdims=True)
             for n in range(2 * n_pop - 1, -1, -1):
                 copy_f(n, 0).start()
                 if n > 0:
                     copy_f(n, 1).start()
 
-    with jax.named_scope("wait_lr"):
-        wait_for(lall.at[half_of], r_l)
-        wait_for(rall.at[half_of], r_r)
-    for d in range(n_pop):
-        right_all[d * mem:(d + 1) * mem, :] = rall[d]
-        left_all[d * mem:(d + 1) * mem, :] = lall[d]
-
     @pl.when(c == 0)
     def _():
         with jax.named_scope("wait_f"):
@@ -595,13 +603,15 @@
         with jax.named_scope("wait_f"):
             wait_for(others, r_f)
 
-    fits[...] = marks[...]
+    fits[0:1] = sum((marks[n] for n in range(1, 2 * n_pop)), marks[0])
+    fits[1:2] = sum((ranked[d] for d in range(1, n_pop)), ranked[0])
     for which in range(2):
         wait_for(send.at[which, 2:units], sent)
     wait_for(send.at[2], sent)
     wait_for(first_v, sent)
     wait_for(lall.at[half_of], sent)
     wait_for(rall.at[half_of], sent)
+    wait_for(ranked.at[half_of], sent)
     for core in range(2):
         @pl.when(c == core)
         def _(core=core):
@@ -641,14 +651,14 @@
     dma = pltpu.SemaphoreType.DMA
     acc = pltpu.VMEM((tok, LANES), F32)
     group = (2 * mem, tok)
-    base, left_all, right_all, fits = pl.pallas_call(
+    base, left_t, right_all, fits = pl.pallas_call(
         functools.partial(kernel, n_pop, n_mp),
         name="es_step",
         out_shape=(
             jax.ShapeDtypeStruct((tok, width), F32),
-            jax.ShapeDtypeStruct((n_pop * mem, rows), BF),
+            jax.ShapeDtypeStruct((rows, n_pop * mem), F32),
             jax.ShapeDtypeStruct((n_pop * mem, width), BF),
-            jax.ShapeDtypeStruct((2 * n_pop, 2, mem), F32),
+            jax.ShapeDtypeStruct((2, n_pop * mem), F32),
         ),
         in_specs=[anywhere] * 8,
         out_specs=[vmem] * 4,
@@ -676,7 +686,9 @@
             pltpu.VMEM((n_mp - 1, pieces, 4, LANES), F32),
             pltpu.VMEM((LANES, LANES), BF),
             pltpu.VMEM((LANES, LANES), BF),
-            pltpu.VMEM((2 * n_pop, 2, mem), F32),
+            pltpu.VMEM((2 * n_pop, 1, LANES), F32),
+            pltpu.VMEM((n_pop * mem, rows), F32),
+            pltpu.VMEM((n_pop, 1, LANES), F32),
             dma((2,)),
             dma((2,)),
             dma,
@@ -685,7 +697,7 @@
             dma((chunks - 1 + pieces,)),
             dma((chunks - 1 + 2 * pieces,)),
         ]
-        + [dma] * 9
+        + [dma] * 10
         + [pltpu.SemaphoreType.REGULAR((3,))],
         compiler_params=pltpu.CompilerParams(
             collective_id=0, has_side_effects=True, vmem_limit_bytes=48 * 1024 * 1024
@@ -698,7 +710,7 @@
     )
     count_all = n_pop * mem
     update, base, fitness = pl.pallas_call(
-        functools.partial(finish, math.sqrt(count_all) / SIGMA, tok * full),
+        functools.partial(finish, n_pop, math.sqrt(count_all) / SIGMA, tok * full),
         name="es_update",
         out_shape=(
             jax.ShapeDtypeStruct((rows, width), F32),
@@ -709,47 +721,39 @@
         out_specs=[anywhere] * 3,
         scratch_shapes=[
             pltpu.VMEM((rows, width), F32),
-            pltpu.VMEM((n_pop * mem, rows), BF),
             pltpu.VMEM((1, mem), F32),
             dma((rows // 128 + 2,)),
         ],
         compiler_params=pltpu.CompilerParams(vmem_limit_bytes=16 * 1024 * 1024),
-    )(left_all, right_all, base, fits)
+    )(left_t, right_all, base, fits)
     return (update, fitness.reshape(mem), base)
 
 
-def finish(scale, count, left_all, right_all, base_in, fits, update, base, fit, held, weighted, fit_v, sems):
+def finish(n_pop, scale, count, left_t, right_all, base_in, fits, update, base, fit, held, fit_v, sems):
     steps = held.shape[0] // 128
     mem = fit_v.shape[1]
-    n_pop = left_all.shape[0] // mem
     members = n_pop * mem
     copies = [
         pltpu.make_async_copy(base_in, base, sems.at[steps]),
         pltpu.make_async_copy(fit_v, fit, sems.at[steps + 1]),
     ]
     copies[0].start()
-    rows_of = [fits[2 * d] + fits[2 * d + 1] for d in range(n_pop)]
-    all_fit = jnp.concatenate([row[0:1] for row in rows_of], axis=0) * (-1.0 / count)
-    all_shaped = jnp.concatenate([row[1:2] for row in rows_of], axis=0)
-    fit_v[...] = all_fit[0:1]
-    copies[1].start()
-    average = jnp.sum(jnp.sum(all_fit, axis=0, keepdims=True), axis=1, keepdims=True) / members
-    centre = all_fit - average
-    deviation = jnp.sqrt(jnp.sum(jnp.sum(centre * centre, axis=0, keepdims=True), axis=1, keepdims=True) / members + 1e-05)
-    weight = all_shaped + centre / deviation / members
-    square = (mem, mem)
-    eye = lax.broadcasted_iota(jnp.int32, square, 0) == lax.broadcasted_iota(jnp.int32, square, 1)
-    for d in range(n_pop):
-        part = slice(d * mem, (d + 1) * mem)
-        upright = jnp.sum(jnp.where(eye, weight[d:d + 1], 0.0), axis=1, keepdims=True)
-        weighted[part, :] = (upright * left_all[part, :].astype(F32)).astype(BF)
+    all_fit = fits[0:1] * (-1.0 / count)
+    centre = all_fit - jnp.sum(all_fit, axis=1, keepdims=True) / members
+    deviation = jnp.sqrt(jnp.sum(centre * centre, axis=1, keepdims=True) / members + 1e-05)
+    weight = fits[1:2] + centre / deviation / members
     for i in range(steps):
         part = slice(i * 128, (i + 1) * 128)
-        held[part, :] = lax.dot_general(
-            weighted[:, part], right_all[...], (((0,), (0,)), ((), ())), preferred_element_type=F32
-        ) * scale
+        weighted = (left_t[part, :] * weight).astype(BF)
+        held[part, :] = jnp.dot(weighted, right_all[...], preferred_element_type=F32) * scale
         copies.append(pltpu.make_async_copy(held.at[part], update.at[part], sems.at[i]))
         copies[-1].start()
+    p = lax.axis_index("pop")
+    mine = jnp.zeros((1, mem), F32)
+    for d in range(n_pop):
+        mine = mine + jnp.where(p == d, 1.0, 0.0) * all_fit[:, d * mem:(d + 1) * mem]
+    fit_v[...] = mine
+    copies[1].start()
     for item in copies:
         item.wait()
 

time: 39.4 us -> 38.6 us (0.980)
  Pallas kernels: 38.5 us -> 37.8 us
    pallas_call x1, Pallas kernels: 35.9 us -> 35.3 us  [fused_shards(): pl.pallas_call(functools.partial(kernel, n_pop, n_mp), name='es_step', ou...]
where the time goes in v5:
time: 38.6 us; the launch traced here: 38.4 us
  Pallas kernels  37.8 us (98%)
  between operations  0.64 us (2%)
    pallas_call x1, Pallas kernels, fused_shards(): pl.pallas_call(functools.partial(kernel, n_pop, n_mp), name='es_step', ou...  35.3 us
    pallas_call x1, Pallas kernels, fused_shards(): pl.pallas_call(functools.partial(finish, n_pop, math.sqrt(count_all) / SI...  2.41 us

profile of v5, /device:TPU:0, one launch (start us, length us, event | category | flops | bytes accessed | tf_op | source)
XLA Modules:
  0.0 38.4 jit_solution(14459941638320509583)
XLA Ops:
  0.6 35.3 %es_step.1 = (f32[384,1280]{1,0:T(8,128)S(1)}, f32[640,128]{1,0:T(8,128)S(1)}, bf16[128,1280]{1,0:T(8,128)(2,1)S(1)}, f32[2,128]{1,0:T(2,128)S(1)}) custom-call(bf16[384,1280]{1,0:T(8,128)(2,1)} %ctx_h.1, bf16[1280,5120]{1,0:T(8,128)(2,1)} %w_h.1, bf16[384,1280]{1,0:T(8,128)(2,1)} %res_h.1, bf16[384,1280]{1,0:T(8,128)(2,1)} %tgt_h.1, f32[1,5120]{1,0:T(1,128)} %bitcast.3, ...), custom_call_target="tpu_custom_call" | custom-call | tf_op jit(solution)/shard_map/es_step/pallas_call | solution.py:654
  36.0 2.4 %es_update.1 = (f32[640,1280]{1,0:T(8,128)}, f32[384,1280]{1,0:T(8,128)}, f32[1,16]{1,0:T(1,128)}) custom-call(f32[640,128]{1,0:T(8,128)S(1)} %get-tuple-element.10.left_t, bf16[128,1280]{1,0:T(8,128)(2,1)S(1)} %get-tuple-element.11.right_all, f32[384,1280]{1,0:T(8,128)S(1)} %get-tuple-element.12.base_in, f32[2,128]{1,0:T(2,128)S(1)} %get-tuple-element.13.fits), custom_call_target="tpu_custom_call" | custom-call | tf_op jit(solution)/shard_map/es_update/pallas_call | solution.py:712

commit v6 on v5

--- a/solution.py
+++ b/solution.py
@@ -125,7 +125,6 @@
     last = units - 1
     pieces = tok // LANES
     upper = LANES
-    per = mem // 2
     members = mem * n_pop
     p = lax.axis_index("pop")
     q = lax.axis_index("mp")
@@ -232,9 +231,8 @@
     def copy_u(d):
         return remote(ranked.at[0], ranked.at[d], sent, r_u, flip(p, d), q)
 
-    def copy_f(n, core):
-        target = flip(q, 2 * (n % 2)) - c + core
-        return remote(marks.at[0], marks.at[n], sent, r_f, flip(p, n // 2), target)
+    def copy_f(d, core):
+        return remote(marks.at[0], marks.at[d], sent, r_f, flip(p, d), 2 * y + core)
 
     copy_lin = remote(lin, lin_in, sent, r_lin, p, mate)
     copy_far = remote(lin_out, lin_far, sent, r_far, p, across)
@@ -421,8 +419,7 @@
     copy_y(chunks - 1, 1).start()
 
     def spread(slot, value):
-        for j in range(2):
-            lin[j, slot * per:(slot + 1) * per, :] = value[j * per:(j + 1) * per]
+        lin[slot * mem:(slot + 1) * mem, :] = value
 
     with jax.named_scope("early"):
         r_mine = rall[0].astype(F32)
@@ -516,7 +513,7 @@
             copy_end(i).start()
         with jax.named_scope("wait_lin"):
             copy_lin.wait_recv()
-        lin_out[...] = lin[1 - y] + lin_in[1 - y]
+        lin_out[...] = lin[...] + lin_in[...]
         copy_far.start()
 
     def settle_chunk(k, carry):
@@ -560,23 +557,18 @@
             def _():
                 copy_post(i, 2).start()
 
-    others = marks.at[pl.ds(1, 2 * n_pop - 1)]
+    others = marks.at[half_of]
 
     @pl.when(c == 1)
     def _():
         with jax.named_scope("wait_far"):
             copy_far.wait_recv()
-        own = lin[y] + lin_in[y] + lin_far[...]
-        mine = jnp.where(y == 1, 1.0, 0.0)
-
-        def my_members(column):
-            return column[0:per] + mine * (column[per:mem] - column[0:per])
-
-        lifted = own[0:per] * (SIGMA / math.sqrt(full))
+        own = lin_out[...] + lin_far[...]
+        lifted = own[0:mem] * (SIGMA / math.sqrt(full))
         lifted2 = lifted * lifted
-        extra_s = 2.0 * lifted * own[2 * per:3 * per] + lifted2 * my_members(norm_r)
-        extra_a = 2.0 * lifted * own[3 * per:4 * per] + lifted2 * my_members(norm_gr)
-        extra_e = lifted * own[per:2 * per]
+        extra_s = 2.0 * lifted * own[2 * mem:3 * mem] + lifted2 * norm_r
+        extra_a = 2.0 * lifted * own[3 * mem:4 * mem] + lifted2 * norm_gr
+        extra_e = lifted * own[mem:2 * mem]
         with jax.named_scope("wait_post"):
             wait_for(post_in, r_post)
         with jax.named_scope("errors"):
@@ -585,13 +577,13 @@
             inverse = lax.rsqrt(meansq + EPSILON)
             errors = inverse * inverse * (late[1:2] + extra_a) - 2.0 * inverse * (late[2:3] + extra_e) + late[3:4]
             summed = jnp.sum(errors, axis=1, keepdims=True)
-            spot = lax.broadcasted_iota(jnp.int32, (per, LANES), 0) + (p * mem + y * per)
-            here = lax.broadcasted_iota(jnp.int32, (per, LANES), 1) == spot
+            spot = lax.broadcasted_iota(jnp.int32, (mem, LANES), 0) + p * mem
+            here = lax.broadcasted_iota(jnp.int32, (mem, LANES), 1) == spot
             marks[0] = jnp.sum(jnp.where(here, summed, 0.0), axis=0, keepdims=True)
-            for n in range(2 * n_pop - 1, -1, -1):
-                copy_f(n, 0).start()
-                if n > 0:
-                    copy_f(n, 1).start()
+            for d in range(n_pop - 1, -1, -1):
+                copy_f(d, 0).start()
+                if d > 0:
+                    copy_f(d, 1).start()
 
     @pl.when(c == 0)
     def _():
@@ -603,7 +595,7 @@
         with jax.named_scope("wait_f"):
             wait_for(others, r_f)
 
-    fits[0:1] = sum((marks[n] for n in range(1, 2 * n_pop)), marks[0])
+    fits[0:1] = sum((marks[d] for d in range(1, n_pop)), marks[0])
     fits[1:2] = sum((ranked[d] for d in range(1, n_pop)), ranked[0])
     for which in range(2):
         wait_for(send.at[which, 2:units], sent)
@@ -650,7 +642,7 @@
     vmem = pl.BlockSpec(memory_space=pltpu.VMEM)
     dma = pltpu.SemaphoreType.DMA
     acc = pltpu.VMEM((tok, LANES), F32)
-    group = (2 * mem, tok)
+    group = pltpu.VMEM((4 * mem, tok), F32)
     base, left_t, right_all, fits = pl.pallas_call(
         functools.partial(kernel, n_pop, n_mp),
         name="es_step",
@@ -678,15 +670,12 @@
             pltpu.VMEM((n_pop, mem, rows), BF),
             pltpu.VMEM((n_pop, mem, width), BF),
             acc, acc, acc, acc,
-            pltpu.VMEM((2,) + group, F32),
-            pltpu.VMEM((2,) + group, F32),
-            pltpu.VMEM(group, F32),
-            pltpu.VMEM(group, F32),
+            group, group, group, group,
             pltpu.VMEM((pieces, 4, LANES), F32),
             pltpu.VMEM((n_mp - 1, pieces, 4, LANES), F32),
             pltpu.VMEM((LANES, LANES), BF),
             pltpu.VMEM((LANES, LANES), BF),
-            pltpu.VMEM((2 * n_pop, 1, LANES), F32),
+            pltpu.VMEM((n_pop, 1, LANES), F32),
             pltpu.VMEM((n_pop * mem, rows), F32),
             pltpu.VMEM((n_pop, 1, LANES), F32),
             dma((2,)),

time: 38.6 us -> 38 us (0.984)
  Pallas kernels: 37.8 us -> 37.2 us
    pallas_call x1, Pallas kernels: 35.3 us -> 34.8 us  [fused_shards(): pl.pallas_call(functools.partial(kernel, n_pop, n_mp), name='es_step', ou...]
where the time goes in v6:
time: 38 us; the launch traced here: 37.8 us
  Pallas kernels  37.2 us (98%)
  between operations  0.64 us (2%)
    pallas_call x1, Pallas kernels, fused_shards(): pl.pallas_call(functools.partial(kernel, n_pop, n_mp), name='es_step', ou...  34.8 us
    pallas_call x1, Pallas kernels, fused_shards(): pl.pallas_call(functools.partial(finish, n_pop, math.sqrt(count_all) / SI...  2.41 us

profile of v6, /device:TPU:0, one launch (start us, length us, event | category | flops | bytes accessed | tf_op | source)
XLA Modules:
  0.0 37.8 jit_solution(13445767218709413197)
XLA Ops:
  0.6 34.8 %es_step.1 = (f32[384,1280]{1,0:T(8,128)S(1)}, f32[640,128]{1,0:T(8,128)S(1)}, bf16[128,1280]{1,0:T(8,128)(2,1)S(1)}, f32[2,128]{1,0:T(2,128)S(1)}) custom-call(bf16[384,1280]{1,0:T(8,128)(2,1)} %ctx_h.1, bf16[1280,5120]{1,0:T(8,128)(2,1)} %w_h.1, bf16[384,1280]{1,0:T(8,128)(2,1)} %res_h.1, bf16[384,1280]{1,0:T(8,128)(2,1)} %tgt_h.1, f32[1,5120]{1,0:T(1,128)} %bitcast.3, ...), custom_call_target="tpu_custom_call" | custom-call | tf_op jit(solution)/shard_map/es_step/pallas_call | solution.py:646
  35.4 2.4 %es_update.1 = (f32[640,1280]{1,0:T(8,128)}, f32[384,1280]{1,0:T(8,128)}, f32[1,16]{1,0:T(1,128)}) custom-call(f32[640,128]{1,0:T(8,128)S(1)} %get-tuple-element.10.left_t, bf16[128,1280]{1,0:T(8,128)(2,1)S(1)} %get-tuple-element.11.right_all, f32[384,1280]{1,0:T(8,128)S(1)} %get-tuple-element.12.base_in, f32[2,128]{1,0:T(2,128)S(1)} %get-tuple-element.13.fits), custom_call_target="tpu_custom_call" | custom-call | tf_op jit(solution)/shard_map/es_update/pallas_call | solution.py:701

commit v7 on v6

--- a/solution.py
+++ b/solution.py
@@ -124,7 +124,9 @@
     units = width // LANES
     last = units - 1
     pieces = tok // LANES
-    upper = LANES
+    upper = 96
+    low = (tok - upper) // 2
+    cuts = [(0, upper), (upper, upper + low), (upper + low, tok)]
     members = mem * n_pop
     p = lax.axis_index("pop")
     q = lax.axis_index("mp")
@@ -196,8 +198,10 @@
         cols = pl.ds(2 * k, 2)
         return remote(send.at[0, cols], recv.at[0, cols], sent, r_a.at[pieces + k - 1], p, mate)
 
+    tail = slice(0, LANES)
+
     def strip(i):
-        return pl.ds(i * LANES, LANES)
+        return slice(*cuts[i])
 
     def copy_a0(i):
         return remote(send.at[0, 0:2, strip(i)], recv.at[0, 0:2, strip(i)], sent, r_a.at[i], p, mate)
@@ -213,8 +217,8 @@
         part = slice(i * LANES, (i + 1) * LANES)
         return remote(send.at[1, last, part], recv.at[1, last, part], sent, r_y.at[pieces + chunks - 1 + i], p, across)
 
-    copy_swap = remote(send.at[1, last, strip(0)], swap_in, sent, r_swap, p, mate)
-    copy_swapped = remote(swap, recv.at[1, last, strip(0)], sent, r_y.at[pieces + chunks - 1], p, diagonal)
+    copy_swap = remote(send.at[1, last, tail], swap_in, sent, r_swap, p, mate)
+    copy_swapped = remote(swap, recv.at[1, last, tail], sent, r_y.at[pieces + chunks - 1], p, diagonal)
 
     def copy_b(k):
         cols = pl.ds(2 * k, 2)
@@ -256,23 +260,33 @@
     top = jnp.dot(ctx[0:upper, :], w_v[1 - c, 0], preferred_element_type=F32).astype(BF)
     first_v[0] = top[:, :LANES]
     first_v[1] = top[:, LANES:]
+    def strip_product(s, i):
+        return jnp.dot(ctx[strip(i), :], w_v[s, 0], preferred_element_type=F32)
+
+    def prepare(i):
+        value = strip_product(0, i).astype(BF)
+        send[0, 0, strip(i)] = value[:, :LANES]
+        send[0, 1, strip(i)] = value[:, LANES:]
+
+    def give(i):
+        prepare(i)
+        copy_a0(i).start()
+
+    @pl.when((c == 1) & (y == 0))
+    def _():
+        locals_[1].wait()
+        prepare(1)
+
     with jax.named_scope("barrier"):
         pl.semaphore_wait(barrier, 6)
     copy_top.start()
     signal(rounds.at[0], flip(p, 1), q)
     for item in w_step(0, True):
         item.start()
-    locals_[1].wait()
-
-    def strip_product(s, i):
-        rows_i = slice(i * LANES, (i + 1) * LANES)
-        return jnp.dot(ctx[rows_i, :], w_v[s, 0], preferred_element_type=F32)
-
-    def give(i):
-        value = strip_product(0, i).astype(BF)
-        send[0, 0, strip(i)] = value[:, :LANES]
-        send[0, 1, strip(i)] = value[:, LANES:]
-        copy_a0(i).start()
+
+    @pl.when((c == 0) | (y == 1))
+    def _():
+        locals_[1].wait()
 
     def pass_on(i, value):
         send[1, 0, strip(i)] = (value[:, :LANES] + recv[0, 0, strip(i)].astype(F32)).astype(BF)
@@ -293,9 +307,13 @@
         send[1, 0, strip(0)] = first_v[0]
         send[1, 1, strip(0)] = first_v[1]
 
+    @pl.when((c == 1) & (y == 1))
+    def _():
+        prepare(1)
+
     @pl.when(c == 1)
     def _():
-        give(1)
+        copy_a0(1).start()
         give(2)
         send[0, 0, strip(0)] = first_v[0]
         send[0, 1, strip(0)] = first_v[1]
@@ -340,7 +358,7 @@
 
         @pl.when((k + 1 == chunks) & (c == 0))
         def _():
-            send[1, last, strip(0)] = mine[0:LANES, LANES:].astype(BF)
+            send[1, last, tail] = mine[0:LANES, LANES:].astype(BF)
             copy_swap.start()
 
         @pl.when(k + 2 < chunks)
@@ -413,7 +431,7 @@
     @pl.when(c == 1)
     def _():
         copy_swap.wait_recv()
-        swap[...] = (send[0, last, strip(0)].astype(F32) + swap_in[...].astype(F32)).astype(BF)
+        swap[...] = (send[0, last, tail].astype(F32) + swap_in[...].astype(F32)).astype(BF)
         copy_swapped.start()
 
     copy_y(chunks - 1, 1).start()
@@ -463,9 +481,9 @@
     with jax.named_scope("linear"):
         top_rows = mixed(other, 0, BLK)
         top = nt_dot(top_rows[:, :LANES], first_v[0]) + nt_dot(top_rows[:, LANES:], first_v[1])
-        top = top + nt_dot(mixed(other, last * LANES, LANES), send[0, last, strip(0)])
+        late = nt_dot(mixed(other, last * LANES, LANES), send[0, last, tail])
+        top = sum(jnp.concatenate([v, jnp.zeros((3 * mem, tok - v.shape[1]), F32)], axis=1) for v in (top, late))
         top = top * jnp.where(c == 1, 1.0, 0.0)
-        top = jnp.concatenate([top, jnp.zeros((3 * mem, tok - upper), F32)], axis=1)
         carry = (top[0:mem], top[mem:2 * mem] + top[2 * mem:3 * mem])
         crossed, crossed_g = lax.fori_loop(0, chunks, linear, carry)
         spread(2, crossed)
@@ -665,8 +683,8 @@
             pltpu.VMEM((1, mem), jnp.int32),
             pltpu.VMEM((3, units, tok, LANES), BF),
             pltpu.VMEM((3, units, tok, LANES), BF),
-            pltpu.VMEM((2, LANES, LANES), BF),
-            pltpu.VMEM((2, 2, LANES, LANES), BF),
+            pltpu.VMEM((2, 96, LANES), BF),
+            pltpu.VMEM((2, 2, 96, LANES), BF),
             pltpu.VMEM((n_pop, mem, rows), BF),
             pltpu.VMEM((n_pop, mem, width), BF),
             acc, acc, acc, acc,

time: 38 us -> 37.9 us (level)
  no operation moved by 1% of the time
where the time goes in v7:
time: 37.9 us; the launch traced here: 37.7 us
  Pallas kernels  37.1 us (98%)
  between operations  0.64 us (2%)
    pallas_call x1, Pallas kernels, fused_shards(): pl.pallas_call(functools.partial(kernel, n_pop, n_mp), name='es_step', ou...  34.6 us
    pallas_call x1, Pallas kernels, fused_shards(): pl.pallas_call(functools.partial(finish, n_pop, math.sqrt(count_all) / SI...  2.41 us

profile of v7, /device:TPU:0, one launch (start us, length us, event | category | flops | bytes accessed | tf_op | source)
XLA Modules:
  0.0 37.7 jit_solution(11630953321827606924)
XLA Ops:
  0.6 34.6 %es_step.1 = (f32[384,1280]{1,0:T(8,128)S(1)}, f32[640,128]{1,0:T(8,128)S(1)}, bf16[128,1280]{1,0:T(8,128)(2,1)S(1)}, f32[2,128]{1,0:T(2,128)S(1)}) custom-call(bf16[384,1280]{1,0:T(8,128)(2,1)} %ctx_h.1, bf16[1280,5120]{1,0:T(8,128)(2,1)} %w_h.1, bf16[384,1280]{1,0:T(8,128)(2,1)} %res_h.1, bf16[384,1280]{1,0:T(8,128)(2,1)} %tgt_h.1, f32[1,5120]{1,0:T(1,128)} %bitcast.3, ...), custom_call_target="tpu_custom_call" | custom-call | tf_op jit(solution)/shard_map/es_step/pallas_call | solution.py:664
  35.3 2.4 %es_update.1 = (f32[640,1280]{1,0:T(8,128)}, f32[384,1280]{1,0:T(8,128)}, f32[1,16]{1,0:T(1,128)}) custom-call(f32[640,128]{1,0:T(8,128)S(1)} %get-tuple-element.10.left_t, bf16[128,1280]{1,0:T(8,128)(2,1)S(1)} %get-tuple-element.11.right_all, f32[384,1280]{1,0:T(8,128)S(1)} %get-tuple-element.12.base_in, f32[2,128]{1,0:T(2,128)S(1)} %get-tuple-element.13.fits), custom_call_target="tpu_custom_call" | custom-call | tf_op jit(solution)/shard_map/es_update/pallas_call | solution.py:719
